TPU v7x, 256 devices: a whole 4x4x8 slice. The times are simulated.
256 devices in a mesh: dp: 4 (over z_lo), ctx: 64 (over z_hi, x, y, core).
Axes of the slice: x: 4, y: 4, z: 8 (z_hi: 2, z_lo: 4; z = z_hi * 4 + z_lo), core: 2. Of those that a mesh axis runs over, the one named last changes fastest.
Arguments:
- inputs: bfloat16 [4, 16384, 4096], P('dp', 'ctx'), may hold values from -16 to 16
- value_weight: bfloat16 [4096, 512], P('ctx'), may hold values from -0.09375 to 0.09375
- query_states: bfloat16 [4, 16384, 2048], P('dp', 'ctx'), may hold values from -40 to 40
- key_states: bfloat16 [4, 16384, 512], P('dp', 'ctx'), may hold values from -6 to 6
- value_states: bfloat16 [4, 16384, 512], P('dp', 'ctx'), may hold values from -6 to 6
- attention_out: bfloat16 [4, 16384, 2048], P('dp', 'ctx'), may hold values from -4 to 4
- out_grad: bfloat16 [4, 16384, 2048], P('dp', 'ctx'), may hold values from -6 to 6
- segment_ids: int32 [4, 16384], P('dp', 'ctx'), may hold values from 0 to 31, never falling along the last dimension, each value on 1 to 4096 neighbouring positions
Outputs:
- query_grad: bfloat16 [4, 16384, 2048], P('dp', 'ctx')
- key_grad: bfloat16 [4, 16384, 512], P('dp', 'ctx')
- input_grad: bfloat16 [4, 16384, 4096], P('dp', 'ctx')
- weight_grad: float32 [4096, 512], P('ctx')
Inputs may be any that keep to these rules, and one draw needn't show every extreme that they name: `segment_ids`: along each sequence the ids never fall; each record holds 1 to 4096 tokens and one holds exactly 4096.
All inputs are finite; a program needn't handle non-finite values.
Results may differ from a plain program's by a relative error of at most 0.0057.
Values may be sent and summed in bfloat16 or wider, within the bound.
A program may use at most 128 MiB of HBM per device.

v0:
```python
import math

import jax
import jax.numpy as jnp
from jax import lax
from jax.sharding import PartitionSpec as P

HQ = 16
KVH = 4
DH = 128
W = 2048


def carried_in(value, axis, combine, identity):
    peers, here = (lax.axis_size(axis), lax.axis_index(axis))
    everything = jax.tree.map(lambda part: lax.all_gather(part, axis), value)
    start = jax.tree.map(
        lambda part, zero: jnp.broadcast_to(jnp.asarray(zero, part.dtype), part.shape),
        value,
        identity,
    )

    def turn(k, before):
        reached = k < here
        new = combine(before, jax.tree.map(lambda part: part[k], everything))
        return jax.tree.map(lambda a, b: jnp.where(reached, a, b), new, before)

    return lax.fori_loop(0, peers, turn, start)


def passed_along(block, axis, distance):
    devices = range(lax.axis_size(axis))
    route = [(i - distance, i) for i in devices if i - distance in devices]
    return lax.ppermute(block, axis, route)


def link_records(earlier, later):
    first_early, last_early, start_early, whole_early, empty_early = earlier
    first_late, last_late, start_late, whole_late, empty_late = later
    joined = last_early == first_late
    start_merged = jnp.where((whole_late == 1) & joined, start_early, start_late)
    whole_merged = jnp.where((whole_early == 1) & (whole_late == 1) & joined, 1, 0).astype(
        jnp.int32
    )
    merged = (first_early, last_late, start_merged, whole_merged, jnp.zeros_like(empty_early))
    return tuple(
        (
            jnp.where(
                empty_early == 1, late_item, jnp.where(empty_late == 1, early_item, merged_item)
            )
            for early_item, late_item, merged_item in zip(earlier, later, merged)
        )
    )


def attend_group(operands, live_mask, factor):
    query_group, key_group, value_group, grad_group, output_group = operands
    scores = (
        jnp.einsum("gqd,kd->gqk", query_group, key_group, preferred_element_type=jnp.float32)
        * factor
    )
    scores = jnp.where(live_mask[None], scores, -1e30)
    row_max = jnp.max(scores, axis=-1, keepdims=True)
    exp_score = jnp.exp(scores - row_max)
    prob_full = exp_score / jnp.sum(exp_score, axis=-1, keepdims=True)
    prob_low = prob_full.astype(jnp.bfloat16)
    row_delta = jnp.sum(
        grad_group.astype(jnp.float32) * output_group.astype(jnp.float32), axis=-1, keepdims=True
    )
    prob_grad = jnp.einsum(
        "gqd,kd->gqk", grad_group, value_group, preferred_element_type=jnp.float32
    )
    score_grad = (prob_full * (prob_grad - row_delta)).astype(jnp.bfloat16)
    query_part = (
        jnp.einsum("gqk,kd->gqd", score_grad, key_group, preferred_element_type=jnp.float32)
        * factor
    )
    key_part = (
        jnp.einsum("gqk,gqd->kd", score_grad, query_group, preferred_element_type=jnp.float32)
        * factor
    )
    value_part = jnp.einsum("gqk,gqd->kd", prob_low, grad_group, preferred_element_type=jnp.float32)
    return (query_part, key_part, value_part)


def attend_tail(factor, operands):
    query_heads, key_heads, value_heads, grad_heads, output_heads, live_mask = operands
    query_part, key_part, value_part = lax.map(
        lambda head_parts: attend_group(head_parts, live_mask, factor),
        (query_heads, key_heads, value_heads, grad_heads, output_heads),
    )
    return (query_part, key_part, value_part)


def on_device(
    inputs,
    value_weight,
    query_states,
    key_states,
    value_states,
    attention_out,
    out_grad,
    segment_ids,
):
    tok_rows = query_states.shape[1]
    span_blocks = W // tok_rows
    group_size = HQ // KVH
    width_kv = KVH * DH
    factor = 1.0 / math.sqrt(DH)
    window_rows = (span_blocks + 1) * tok_rows
    input_rows = inputs[0]
    values = value_states[0]
    seg_local = segment_ids[0]
    device_index = lax.axis_index("ctx")
    offset = device_index * tok_rows
    before = jnp.sum((seg_local[None, :] < seg_local[:, None]).astype(jnp.int32), axis=1)
    first_id = seg_local[0]
    last_id = seg_local[-1]
    summary = (
        first_id,
        last_id,
        offset + before[-1],
        (first_id == last_id).astype(jnp.int32),
        jnp.zeros((), jnp.int32),
    )
    identity = tuple((jnp.full((), filler, jnp.int32) for filler in (0, 0, 0, 1, 1)))
    prior = carried_in(summary, "ctx", link_records, identity)
    carried = (before == 0) & (prior[4] == 0) & (prior[1] == first_id)
    starts = jnp.where(carried, prior[2], offset + before)
    kv_block = jnp.stack([key_states[0], values])
    blank_window = jnp.zeros((2, window_rows, width_kv), jnp.bfloat16)
    blank_window = lax.dynamic_update_slice_in_dim(
        blank_window, kv_block, span_blocks * tok_rows, 1
    )

    def pass_on(hop_number, carry):
        moving, filled = carry
        moving = passed_along(moving, "ctx", 1)
        filled = lax.dynamic_update_slice_in_dim(
            filled, moving, (span_blocks - hop_number) * tok_rows, 1
        )
        return (moving, filled)

    window = lax.fori_loop(1, span_blocks + 1, pass_on, (kv_block, blank_window))[1]
    key_base = offset - span_blocks * tok_rows
    key_pos = key_base + jnp.arange(window_rows, dtype=jnp.int32)
    query_pos = offset + jnp.arange(tok_rows, dtype=jnp.int32)
    live_mask = (
        (key_pos[None, :] >= starts[:, None])
        & (key_pos[None, :] <= query_pos[:, None])
        & (key_pos[None, :] > query_pos[:, None] - W)
    )
    query_heads = query_states[0].reshape(tok_rows, KVH, group_size, DH).transpose(1, 2, 0, 3)
    grad_heads = out_grad[0].reshape(tok_rows, KVH, group_size, DH).transpose(1, 2, 0, 3)
    output_heads = attention_out[0].reshape(tok_rows, KVH, group_size, DH).transpose(1, 2, 0, 3)
    key_heads = window[0].reshape(window_rows, KVH, DH).transpose(1, 0, 2)
    value_heads = window[1].reshape(window_rows, KVH, DH).transpose(1, 0, 2)
    operands = (query_heads, key_heads, value_heads, grad_heads, output_heads, live_mask)
    query_part, key_part, value_part = attend_tail(factor, operands)
    query_grad = query_part.transpose(2, 0, 1, 3).reshape(1, tok_rows, HQ * DH).astype(jnp.bfloat16)
    grads = jnp.stack(
        [
            key_part.transpose(1, 0, 2).reshape(window_rows, width_kv),
            value_part.transpose(1, 0, 2).reshape(window_rows, width_kv),
        ]
    )

    def return_step(hop_number, carried_sum):
        moved = passed_along(carried_sum, "ctx", -1)
        return moved + lax.dynamic_slice_in_dim(grads, hop_number * tok_rows, tok_rows, 1)

    totals = lax.fori_loop(1, span_blocks + 1, return_step, grads[:, :tok_rows])
    key_grad = totals[0].astype(jnp.bfloat16)[None]
    value_delta = totals[1].astype(jnp.bfloat16)
    input_grad = jnp.einsum(
        "tk,rk->tr",
        value_delta,
        lax.all_gather(value_weight, "ctx", axis=0, tiled=True),
        preferred_element_type=jnp.float32,
    )
    input_grad = input_grad.astype(jnp.bfloat16)[None]
    weight_share = lax.psum_scatter(
        jnp.einsum("tr,tk->rk", input_rows, value_delta, preferred_element_type=jnp.float32),
        "ctx",
        scatter_dimension=0,
        tiled=True,
    )
    weight_grad = lax.psum(weight_share, "dp")
    return (query_grad, key_grad, input_grad, weight_grad)


def solution(mesh):
    placed = (
        P("dp", "ctx", None),
        P("ctx", None),
        P("dp", "ctx", None),
        P("dp", "ctx", None),
        P("dp", "ctx", None),
        P("dp", "ctx", None),
        P("dp", "ctx", None),
        P("dp", "ctx"),
    )
    return jax.shard_map(
        on_device,
        mesh=mesh,
        in_specs=placed,
        out_specs=(
            P("dp", "ctx", None),
            P("dp", "ctx", None),
            P("dp", "ctx", None),
            P("ctx", None),
        ),
        check_vma=False,
    )
```

profile of v0, /device:TPU:39, one launch (start us, length us, event | category | flops | bytes accessed | tf_op | source)
XLA Modules:
  0.0 1695.6 jit_solution(13102222631023237591)
XLA Ops:
  18.7 18.7 %all-reduce.6 = (s32[64]{0:T(128)S(1)}, s32[64]{0:T(128)S(1)}, s32[64]{0:T(128)S(1)}, s32[64]{0:T(128)S(1)}, s32[64]{0:T(128)S(1)}) all-reduce(s32[64]{0:T(128)S(1)} %bitcast_dynamic-update-slice_fusion.1, s32[64]{0:T(128)S(1)} %dynamic-update-slice.1, s32[64]{0:T(128)S(1)} %dynamic-update-slice.2, ...), channel_id=2, replica_groups=mesh['dp'=4,'ctx'=64] {'ctx'}, use_global_device_ids=true, to_apply=%add.1 | all-reduce | flops 320 | bytes 2560 | tf_op jit(solution)/shard_map/all_gather | solution.py:16
  37.3 521.7 %while.60 = (s32[]{:T(128)}, s32[]{:T(128)}, s32[]{:T(128)}, s32[]{:T(128)}, s32[]{:T(128)}, /*index=5*/s32[64]{0:T(128)S(1)}, s32[64]{0:T(128)S(1)}, s32[64]{0:...) while((s32[]{:T(128)}, s32[]{:T(128)}, s32[]{:T(128)}, ...), condition=%wide.region_4.5_spmd, body=%wide.region_3.4_spmd.sunk | while | flops 18 | bytes 363 | solution.py:28
  561.6 2.5 dynamic_update_slice.21
  564.0 103.1 %while.61 = (s32[]{:T(128)}, bf16[2,256,512]{2,1,0:T(8,128)(2,1)S(1)}, bf16[2,2304,512]{2,1,0:T(8,128)(2,1)}, s32[]{:T(128)}, s32[]{:T(128)}, /*index=5*/s32[]{:T(128)}, s32[]{:T(128)}, s32[]{:T(128)}) while((s32[]{:T(128)}, bf16[2,256,512]{2,1,0:T(8,128)(2,1)S(1)}, bf16[2,2304,512]{2,1,0:T(8,128)(2,1)}, s32[]{:T(128)}, s32[]{:T(128)}, ...), condition=%wide.region_1.2_spmd, body=%wide.region_0.0_spmd.sunk | while | flops 7 | bytes 4194491 | solution.py:144
  564.0 6.3 collective-permute-start
  570.3 6.1 collective-permute-done
  577.3 4.4 collective-permute-start
  581.7 6.1 collective-permute-done
  588.7 4.4 collective-permute-start
  593.1 6.1 collective-permute-done
  600.1 4.4 collective-permute-start
  604.5 7.9 collective-permute-done
  613.2 2.6 collective-permute-start
  615.9 10.0 collective-permute-done
  628.7 10.7 collective-permute-done
  642.1 10.7 collective-permute-done
  655.6 10.7 collective-permute-done
  667.2 6.7 copy.55
  673.9 4.9 fusion.82
  684.7 144.7 %while.63 = (s32[]{:T(128)}, bf16[4,4,256,128]{3,2,1,0:T(8,128)(2,1)}, f32[4,2304,128]{1,2,0:T(8,128)}, f32[4,2304,128]{1,2,0:T(8,128)}, bf16[4,4,256,128]{2,3,1...) while((s32[]{:T(128)}, ...), condition=%wide.region_9.10_spmd.clone, body=%wide.region_5.9_spmd.clone.sunk | while | flops 3658453504 | bytes 69966016 | solution.py:88
  687.3 8.5 fusion.117
  695.9 5.4 multiply_convert_fusion.2
  703.4 3.4 fusion.119
  709.6 4.6 fusion.118
  714.1 6.8 fusion.120
  723.4 8.6 fusion.117
  732.0 5.4 multiply_convert_fusion.2
  739.5 3.4 fusion.119
  745.7 4.6 fusion.118
  750.3 6.8 fusion.120
  759.5 8.6 fusion.117
  768.1 5.4 multiply_convert_fusion.2
  775.7 3.4 fusion.119
  781.8 4.6 fusion.118
  786.4 6.8 fusion.120
  795.7 8.6 fusion.117
  804.2 5.4 multiply_convert_fusion.2
  811.8 3.4 fusion.119
  818.0 4.6 fusion.118
  822.5 6.8 fusion.120
  829.3 8.8 pad_maximum_fusion
  839.7 193.3 %while.62 = (s32[]{:T(128)}, f32[2,256,512]{2,1,0:T(8,128)}, f32[2,2304,512]{1,2,0:T(8,128)}, s32[]{:T(128)}, s32[]{:T(128)}, /*index=5*/s32[]{:T(128)}, s32[]{:T(128)}) while((s32[]{:T(128)}, f32[2,256,512]{2,1,0:T(8,128)}, f32[2,2304,512]{1,2,0:T(8,128)}, s32[]{:T(128)}, s32[]{:T(128)}, /*index=5*/s32[]{:T(128)}, s32[]{:T(128)}) %tuple.122), condition=%wide.region_11.12_spmd, body=%wide.region_10.11_spmd.sunk | while | flops 262150 | bytes 11534503 | solution.py:172
  839.7 11.2 collective-permute-start.1
  856.2 2.4 add.167
  858.6 9.3 collective-permute-start.1
  871.7 3.3 collective-permute-done.1
  875.0 2.4 add.167
  877.4 11.4 collective-permute-start.1
  892.6 5.9 collective-permute-done.1
  898.5 2.4 add.167
  901.0 8.8 collective-permute-start.1
  913.6 7.0 collective-permute-done.1
  920.5 2.4 add.167
  922.9 7.7 collective-permute-start.1
  934.5 13.7 collective-permute-done.1
  956.4 13.8 collective-permute-done.1
  978.4 25.2 %collective-permute-done.1 = f32[2,256,512]{2,1,0:T(8,128)} collective-permute-done((f32[2,256,512]{2,1,0:T(8,128)}, f32[2,256,512]{2,1,0:T(8,128)}, u32[]{:S(2)}, u32[]{:S(2)}) %collective-permute-start.1) | collective-permute-done | bytes 1048608 | tf_op jit(solution)/shard_map/while/body/eval_jaxpr/ppermute | solution.py:34
  1011.7 18.9 %collective-permute-done.1 = f32[2,256,512]{2,1,0:T(8,128)} collective-permute-done((f32[2,256,512]{2,1,0:T(8,128)}, f32[2,256,512]{2,1,0:T(8,128)}, u32[]{:S(2)}, u32[]{:S(2)}) %collective-permute-start.1) | collective-permute-done | bytes 1048608 | tf_op jit(solution)/shard_map/while/body/eval_jaxpr/ppermute | solution.py:34
  1033.0 5.6 convolution_bitcast_fusion.1
  1038.5 9.0 copy.72
  1053.8 469.7 %reduce-scatter.4.cloned.1.call-done = f32[64,512]{1,0:T(8,128)} async-done(((f32[4096,512]{1,0:T(8,128)}), f32[64,512]{1,0:T(8,128)}) %reduce-scatter.4.cloned.1.call-update) | async-done | bytes 131088
  1525.3 118.1 %all-gather.4.cloned.1.call-done = bf16[4096,512]{1,0:T(8,128)(2,1)} async-done(((bf16[64,512]{1,0:T(8,128)(2,1)}), bf16[4096,512]{1,0:T(8,128)(2,1)}) %all-gather.4.cloned.1.call-update) | async-done | bytes 4194320 | tf_op jit(solution)/shard_map/all_gather | solution.py:178
  1643.4 5.0 fusion.71
  1648.3 39.1 %all-reduce.9.cloned.1.call-done = f32[64,512]{0,1:T(8,128)} async-done(((f32[64,512]{0,1:T(8,128)}), f32[64,512]{0,1:T(8,128)}) %all-reduce.9.cloned.1.call-update) | async-done | bytes 131088 | tf_op jit(solution)/shard_map/psum | solution.py:188
  (453 shorter events, 312.9 us)
Async XLA Ops:
  7.2 1025.8 %copy-start = (bf16[1,256,4096]{2,1,0:T(8,128)(2,1)S(1)}, bf16[1,256,4096]{2,1,0:T(8,128)(2,1)}, u32[]{:S(2)}) copy-start(bf16[1,256,4096]{2,1,0:T(8,128)(2,1)} %param.16) | copy-start | bytes 6291460
  7.2 1516.3 %reduce-scatter.4.cloned.1.call-start = ((), (), s32[]{:S(2)}) async-start(), calls=%async_computation.3 | async-start | bytes 8519680
  564.0 12.4 collective-permute-start
  577.3 10.5 collective-permute-start
  588.7 10.5 collective-permute-start
  600.1 12.2 collective-permute-start
  613.2 12.6 collective-permute-start
  626.7 12.6 collective-permute-start
  640.2 12.6 collective-permute-start
  653.7 12.6 collective-permute-start
  673.9 4.9 copy-start.5
  687.3 8.6 copy-start.4
  701.3 2.1 copy-start.1
  723.4 8.6 copy-start.4
  737.4 2.1 copy-start.1
  759.5 8.6 copy-start.4
  773.5 2.1 copy-start.1
  795.6 8.6 copy-start.4
  809.6 2.1 copy-start.1
  829.3 8.9 copy-start.2
  829.3 9.0 copy-start.3
  839.7 16.4 collective-permute-start.1
  858.6 16.4 collective-permute-start.1
  877.4 21.2 %collective-permute-start.1 = (f32[2,256,512]{2,1,0:T(8,128)}, f32[2,256,512]{2,1,0:T(8,128)}, u32[]{:S(2)}, u32[]{:S(2)}) collective-permute-start(f32[2,256,512]{2,1,0:T(8,128)} %get-tuple-element.833), channel_id=1, source_target_pairs={{1,0},{2,1},{3,2},{4,3},{5,4},{6,5},{7,6},{8,7},{9,8},{10,9},{11,1... | collective-permute-start | bytes 3145736 | tf_op jit(solution)/shard_map/while/body/eval_jaxpr/ppermute | solution.py:34
  901.0 19.6 %collective-permute-start.1 = (f32[2,256,512]{2,1,0:T(8,128)}, f32[2,256,512]{2,1,0:T(8,128)}, u32[]{:S(2)}, u32[]{:S(2)}) collective-permute-start(f32[2,256,512]{2,1,0:T(8,128)} %get-tuple-element.833), channel_id=1, source_target_pairs={{1,0},{2,1},{3,2},{4,3},{5,4},{6,5},{7,6},{8,7},{9,8},{10,9},{11,1... | collective-permute-start | bytes 3145736 | tf_op jit(solution)/shard_map/while/body/eval_jaxpr/ppermute | solution.py:34
  922.9 25.3 %collective-permute-start.1 = (f32[2,256,512]{2,1,0:T(8,128)}, f32[2,256,512]{2,1,0:T(8,128)}, u32[]{:S(2)}, u32[]{:S(2)}) collective-permute-start(f32[2,256,512]{2,1,0:T(8,128)} %get-tuple-element.833), channel_id=1, source_target_pairs={{1,0},{2,1},{3,2},{4,3},{5,4},{6,5},{7,6},{8,7},{9,8},{10,9},{11,1... | collective-permute-start | bytes 3145736 | tf_op jit(solution)/shard_map/while/body/eval_jaxpr/ppermute | solution.py:34
  950.6 19.6 %collective-permute-start.1 = (f32[2,256,512]{2,1,0:T(8,128)}, f32[2,256,512]{2,1,0:T(8,128)}, u32[]{:S(2)}, u32[]{:S(2)}) collective-permute-start(f32[2,256,512]{2,1,0:T(8,128)} %get-tuple-element.833), channel_id=1, source_target_pairs={{1,0},{2,1},{3,2},{4,3},{5,4},{6,5},{7,6},{8,7},{9,8},{10,9},{11,1... | collective-permute-start | bytes 3145736 | tf_op jit(solution)/shard_map/while/body/eval_jaxpr/ppermute | solution.py:34
  972.6 30.9 %collective-permute-start.1 = (f32[2,256,512]{2,1,0:T(8,128)}, f32[2,256,512]{2,1,0:T(8,128)}, u32[]{:S(2)}, u32[]{:S(2)}) collective-permute-start(f32[2,256,512]{2,1,0:T(8,128)} %get-tuple-element.833), channel_id=1, source_target_pairs={{1,0},{2,1},{3,2},{4,3},{5,4},{6,5},{7,6},{8,7},{9,8},{10,9},{11,1... | collective-permute-start | bytes 3145736 | tf_op jit(solution)/shard_map/while/body/eval_jaxpr/ppermute | solution.py:34
  1005.9 24.6 %collective-permute-start.1 = (f32[2,256,512]{2,1,0:T(8,128)}, f32[2,256,512]{2,1,0:T(8,128)}, u32[]{:S(2)}, u32[]{:S(2)}) collective-permute-start(f32[2,256,512]{2,1,0:T(8,128)} %get-tuple-element.833), channel_id=1, source_target_pairs={{1,0},{2,1},{3,2},{4,3},{5,4},{6,5},{7,6},{8,7},{9,8},{10,9},{11,1... | collective-permute-start | bytes 3145736 | tf_op jit(solution)/shard_map/while/body/eval_jaxpr/ppermute | solution.py:34
  1047.6 595.8 %all-gather.4.cloned.1.call-start = ((), (), s32[]{:S(2)}) async-start(), calls=%async_computation.1 | async-start | bytes 4259840 | tf_op jit(solution)/shard_map/all_gather | solution.py:178
  1048.3 639.0 %all-reduce.9.cloned.1.call-start = ((), (), s32[]{:S(2)}) async-start(), calls=%async_computation.2 | async-start | bytes 524288 | tf_op jit(solution)/shard_map/psum | solution.py:188
Sparse Core Ops, SparseCore 0:
  1047.7 475.7 reduce-scatter.3
  1527.2 116.1 all-gather.3
  1646.0 41.3 all-reduce.8
where the time goes:
time: 1710 us; the launch traced here: 1700 us
  waiting for transfers between devices  785 us (46%)
  loops' own time  327 us (19%)
  local copies, waits for them, and re-layouts  308 us (18%)
  matrix products  126 us (7%)
  starting transfers between devices  82 us (5%)
  other arithmetic  33.3 us (2%)
  blocking collectives  18.7 us (1%)
    unnamed x4, waiting for transfers between devices  470 us
    another operation x1, loops' own time, carried_in(): return lax.fori_loop(0, peers, turn, start)  327 us
    dynamic_slice x320, local copies, waits for them, and re-layouts, turn(): new = combine(before, jax.tree.map(lambda part: part[k], everything))  195 us
    ppermute x16, waiting for transfers between devices, passed_along(): return lax.ppermute(block, axis, route)  157 us
    all_gather x1, waiting for transfers between devices, on_device(): lax.all_gather(value_weight, 'ctx', axis=0, tiled=True)  118 us
    ppermute x16, starting transfers between devices, passed_along(): return lax.ppermute(block, axis, route)  81.9 us
    psum x1, waiting for transfers between devices, on_device(): weight_grad = lax.psum(weight_share, 'dp')  39.1 us
    sub x4, matrix products, attend_group(): exp_score = jnp.exp(scores - row_max)  34.2 us
  transfers between devices with their start and end apart: 19, of which 19 were waited for; matrix products, arithmetic and copies ran while one was open for 3% of the time, Pallas kernels for 0%

commit v1 on v0

v1 whole, which is shorter than its diff:
```python
import math

import jax
import jax.numpy as jnp
from jax import lax
from jax.experimental import pallas as pl
from jax.experimental.pallas import tpu as pltpu
from jax.sharding import PartitionSpec as P

DH = 128
W = 2048
T = 256
CHIP = 2 * T
NK = W // T + 1
WIN = W + CHIP
FACTOR = 1.0 / math.sqrt(DH)
FACTOR2 = FACTOR * math.log2(math.e)
BF = jnp.bfloat16
F32 = jnp.float32
MESH = pl.DeviceIdType.MESH
ANY = pl.BlockSpec(memory_space=pl.ANY)
VM = pl.BlockSpec(memory_space=pltpu.VMEM)
NT = (((1,), (1,)), ((), ()))
NN = (((1,), (0,)), ((), ()))
TN = (((0,), (0,)), ((), ()))


def dot(a, b, dims):
    return lax.dot_general(a, b, dims, preferred_element_type=F32)


def signal(sem, ctx):
    pl.semaphore_signal(sem, inc=1, device_id={"ctx": ctx}, device_id_type=MESH)


def remote(src, dst, send, recv, ctx):
    return pltpu.make_async_remote_copy(
        src_ref=src,
        dst_ref=dst,
        send_sem=send,
        recv_sem=recv,
        device_id={"ctx": ctx},
        device_id_type=MESH,
    )


def gather_kernel(
    q_in, do_in, de_in, k_in, v_in, sg_in, kv_zero, sg_none,
    q_out, do_out, de_out, kv_out, sg_out,
    lsem, psend, precv, asend, arecv, rsend, rrecv,
):
    me = lax.axis_index("ctx")
    core = lax.rem(me, 2)
    other = 1 - core
    y = lax.rem(me // 2, 4)
    partner = me + 1 - 2 * core
    row0 = me - 2 * y
    has_next = me < 56
    has_prev = me >= 8

    barrier = pltpu.get_barrier_semaphore()
    signal(barrier, partner)
    for k in (1, 2, 3):
        signal(barrier, row0 + 2 * lax.rem(y + k, 4))

    @pl.when(has_next)
    def _():
        signal(barrier, me + 8)

    @pl.when(has_prev)
    def _():
        signal(barrier, me - 8)

    pl.semaphore_wait(barrier, 4 + has_next.astype(jnp.int32) + has_prev.astype(jnp.int32))

    rows = pl.ds(pl.multiple_of(core * T, T), T)
    kv_rows = pl.ds(pl.multiple_of(W + core * T, T), T)

    def cols(c, n):
        return pl.ds(pl.multiple_of(c * n, n), n)

    pairs = (
        (lambda c: k_in.at[:, cols(c, 2 * DH)], kv_out.at[0, kv_rows, :]),
        (lambda c: v_in.at[:, cols(c, 2 * DH)], kv_out.at[1, kv_rows, :]),
        (lambda c: sg_in, sg_out.at[4, core]),
        (lambda c: q_in.at[:, cols(c, 8 * DH)], q_out.at[rows, :]),
        (lambda c: do_in.at[:, cols(c, 8 * DH)], do_out.at[rows, :]),
        (lambda c: de_in.at[c], de_out.at[core]),
    )
    swaps = [
        remote(src(other), dst, psend.at[i], precv.at[i], partner)
        for i, (src, dst) in enumerate(pairs)
    ]
    locals_ = [
        pltpu.make_async_copy(src(core), dst, lsem.at[i]) for i, (src, dst) in enumerate(pairs)
    ]
    for i in range(6):
        swaps[i].start()
        locals_[i].start()
    for i in range(3):
        locals_[i].wait()
        swaps[i].wait_recv()

    def slot(s):
        return kv_out.at[:, pl.ds(s * CHIP, CHIP), :], sg_out.at[s]

    own, first = slot(4), slot(0)
    ahead = [remote(own[i], first[i], asend.at[i], arecv.at[i], me + 8) for i in (0, 1)]

    @pl.when(has_next)
    def _():
        ahead[0].start()
        ahead[1].start()

    def along(k, src):
        to = row0 + 2 * lax.rem(y + k, 4)
        dst = slot(4 - k)
        return [
            remote(src[i], dst[i], rsend.at[k - 1, i], rrecv.at[k - 1, i], to) for i in (0, 1)
        ]

    for k in (1, 2, 3):

        @pl.when(y + k < 4)
        def _():
            for copy in along(k, own):
                copy.start()

    @pl.when(has_prev)
    def _():
        ahead[0].wait_recv()
        ahead[1].wait_recv()

    @pl.when(jnp.logical_not(has_prev))
    def _():
        fill = (
            pltpu.make_async_copy(kv_zero, first[0], lsem.at[6]),
            pltpu.make_async_copy(sg_none, first[1], lsem.at[7]),
        )
        for copy in fill:
            copy.start()
        for copy in fill:
            copy.wait()

    for k in (1, 2, 3):

        @pl.when(y + k >= 4)
        def _():
            for copy in along(k, first):
                copy.start()

    for k in (1, 2, 3):
        for copy in along(k, own):
            copy.wait()
    for i in range(3):
        swaps[i].wait_send()
    for i in range(3, 6):
        locals_[i].wait()
        swaps[i].wait()

    @pl.when(has_next)
    def _():
        ahead[0].wait_send()
        ahead[1].wait_send()


def gather(q, do, de, k, v, sg):
    dma = pltpu.SemaphoreType.DMA
    return pl.pallas_call(
        gather_kernel,
        in_specs=[ANY] * 8,
        out_specs=[ANY] * 5,
        out_shape=[
            jax.ShapeDtypeStruct((CHIP, 8 * DH), BF),
            jax.ShapeDtypeStruct((CHIP, 8 * DH), BF),
            jax.ShapeDtypeStruct((2, 8, T), F32),
            jax.ShapeDtypeStruct((2, WIN, 2 * DH), BF),
            jax.ShapeDtypeStruct((5, 2, 8, T), jnp.int32),
        ],
        scratch_shapes=[
            dma((8,)), dma((6,)), dma((6,)), dma((2,)), dma((2,)), dma((3, 2)), dma((3, 2)),
        ],
        compiler_params=pltpu.CompilerParams(collective_id=0, has_side_effects=True),
        name="window_gather",
    )(
        q, do, de, k, v, sg,
        jnp.zeros((2, CHIP, 2 * DH), BF),
        jnp.full((2, 8, T), -1, jnp.int32),
    )


def attend_kernel(
    q_ref, do_ref, de_ref, k_ref, v_ref, sq_ref, sk_ref, dq_ref, dk_ref, dv_ref, bias, s_ref, dk, dv
):
    g, h, t = pl.program_id(0), pl.program_id(1), pl.program_id(2)

    def rows(c):
        return pl.ds(pl.multiple_of(t * T + c * T, T), T)

    @pl.when((g == 0) & (h == 0))
    def _():
        for c in range(NK):
            kpos = lax.broadcasted_iota(jnp.int32, (T, T), 0) + (c * T - W)
            qpos = lax.broadcasted_iota(jnp.int32, (T, T), 1)
            sk = sk_ref[rows(c), :]
            sk = jnp.concatenate([sk, sk], axis=1)
            live = (sk == sq_ref[pl.ds(t, 1), :]) & (kpos <= qpos) & (kpos > qpos - W)
            bias[t, c] = jnp.where(live, 0.0, -1e30)

    @pl.when((h == 0) & (t == 0))
    def _():
        dk[...] = jnp.zeros_like(dk)
        dv[...] = jnp.zeros_like(dv)

    q, do = q_ref[...], do_ref[...]
    top = jnp.full((8, T), -1e30, F32)
    for c in range(NK):
        s = dot(k_ref[0, rows(c), :], q, NT) + bias[t, c]
        s_ref[c] = s
        top = jnp.maximum(top, jnp.max(s.reshape(T // 8, 8, T), axis=0))
    top = jnp.max(top, axis=0, keepdims=True)
    total = jnp.zeros((8, T), F32)
    for c in range(NK):
        e = jnp.exp2((s_ref[c] - top) * FACTOR2)
        s_ref[c] = e
        total = total + jnp.sum(e.reshape(T // 8, 8, T), axis=0)
    inverse = 1.0 / jnp.sum(total, axis=0, keepdims=True)
    delta = de_ref[t, pl.ds(g * 4 + h, 1), :]
    dq = jnp.zeros((T, DH), F32)
    for c in range(NK):
        p = s_ref[c] * inverse
        dv[rows(c), :] += dot(p.astype(BF), do, NN)
        dp = dot(v_ref[0, rows(c), :], do, NT)
        ds = (p * (dp - delta)).astype(BF)
        dk[rows(c), :] += dot(ds, q, NN)
        dq = dq + dot(ds, k_ref[0, rows(c), :], TN)
    dq_ref[...] = (dq * FACTOR).astype(BF)

    @pl.when((h == 3) & (t == 1))
    def _():
        dk_ref[...] = (dk[...] * FACTOR).astype(BF)
        dv_ref[...] = dv[...].astype(BF)


def attend(q, do, de, kv, sq, sk):
    heads = pl.BlockSpec((T, DH), lambda g, h, t: (t, g * 4 + h))
    window = pl.BlockSpec((WIN, DH), lambda g, h, t: (0, g))
    return pl.pallas_call(
        attend_kernel,
        grid=(2, 4, 2),
        in_specs=[
            heads,
            heads,
            pl.BlockSpec((2, 8, T), lambda g, h, t: (0, 0, 0)),
            pl.BlockSpec((1, WIN, DH), lambda g, h, t: (0, 0, g)),
            pl.BlockSpec((1, WIN, DH), lambda g, h, t: (1, 0, g)),
            pl.BlockSpec((2, T), lambda g, h, t: (0, 0)),
            pl.BlockSpec((WIN, 128), lambda g, h, t: (0, 0)),
        ],
        out_specs=[heads, window, window],
        out_shape=[
            jax.ShapeDtypeStruct((CHIP, 8 * DH), BF),
            jax.ShapeDtypeStruct((WIN, 2 * DH), BF),
            jax.ShapeDtypeStruct((WIN, 2 * DH), BF),
        ],
        scratch_shapes=[
            pltpu.VMEM((2, NK, T, T), F32),
            pltpu.VMEM((NK, T, T), F32),
            pltpu.VMEM((WIN, DH), F32),
            pltpu.VMEM((WIN, DH), F32),
        ],
        compiler_params=pltpu.CompilerParams(vmem_limit_bytes=48 << 20),
        cost_estimate=pl.CostEstimate(
            flops=12_000_000_000, bytes_accessed=9_000_000, transcendentals=9_400_000
        ),
        name="attend",
    )(q, do, de, kv, kv, sq, sk)


def scatter_kernel(
    dq_in, dk_in, dv_in,
    dq_out, dk_out, vd_out, vx_out,
    got, part, kept, ahead_buf, total,
    lsem, psend, precv, asend, arecv, rsend, rrecv, xsend, xrecv,
):
    me = lax.axis_index("ctx")
    core = lax.rem(me, 2)
    other = 1 - core
    y = lax.rem(me // 2, 4)
    x = lax.rem(me // 8, 4)
    partner = me + 1 - 2 * core
    row0 = me - 2 * y
    column0 = me - 8 * x
    has_next = me < 56
    has_prev = me >= 8

    def row_peer(k):
        return row0 + 2 * lax.rem(y + k, 4)

    def column_peer(k):
        return column0 + 8 * lax.rem(x + k, 4)

    barrier = pltpu.get_barrier_semaphore()
    signal(barrier, partner)
    for k in (1, 2, 3):
        signal(barrier, row_peer(k))
        signal(barrier, column_peer(k))
    far_next = (x == 3) & has_next
    far_prev = (x == 0) & has_prev

    @pl.when(far_next)
    def _():
        signal(barrier, me + 8)

    @pl.when(far_prev)
    def _():
        signal(barrier, me - 8)

    pl.semaphore_wait(barrier, 7 + far_next.astype(jnp.int32) + far_prev.astype(jnp.int32))

    def half(c):
        return pl.ds(pl.multiple_of(c * T, T), T)

    def cols(c, n):
        return pl.ds(pl.multiple_of(c * n, n), n)

    def slot(ref, s):
        return ref.at[pl.ds(s * CHIP, CHIP), :]

    grads = (dv_in, dk_in)
    sends = [
        [
            remote(slot(grads[j], 4 - k), got.at[j, k - 1], rsend.at[j, k - 1], rrecv.at[j, k - 1], row_peer(4 - k))
            for k in (1, 2, 3)
        ]
        for j in (0, 1)
    ]
    keeps = [
        [pltpu.make_async_copy(slot(grads[j], 4 * i), kept.at[j, i], lsem.at[j, i]) for i in (0, 1)]
        for j in (0, 1)
    ]
    for j in (0, 1):
        for copy in sends[j] + keeps[j]:
            copy.start()
    dq_swap = remote(dq_in.at[half(other), :], dq_out.at[:, cols(core, 8 * DH)], psend.at[2], precv.at[2], partner)
    dq_keep = pltpu.make_async_copy(dq_in.at[half(core), :], dq_out.at[:, cols(core, 8 * DH)], lsem.at[2, 0])
    dq_swap.start()
    dq_keep.start()

    aheads = [
        remote(part.at[j], ahead_buf.at[j], asend.at[j], arecv.at[j], me - 8) for j in (0, 1)
    ]
    tails = []
    for j in (0, 1):
        for copy in keeps[j]:
            copy.wait()
        for copy in sends[j]:
            copy.wait_recv()
        before = kept[j, 0].astype(F32)
        for k in (1, 2, 3):
            before = before + jnp.where(y + k >= 4, got[j, k - 1].astype(F32), 0.0)
        part[j] = before.astype(BF)

        @pl.when(has_prev)
        def _():
            aheads[j].start()

    for j in (0, 1):
        mine = kept[j, 1].astype(F32)
        for k in (1, 2, 3):
            mine = mine + jnp.where(y + k < 4, got[j, k - 1].astype(F32), 0.0)

        @pl.when(has_next)
        def _():
            aheads[j].wait_recv()

        @pl.when(jnp.logical_not(has_next))
        def _():
            ahead_buf[j] = jnp.zeros_like(ahead_buf[j])

        total[j] = (mine + ahead_buf[j].astype(F32)).astype(BF)
        out = (vd_out, dk_out)[j]
        swap = remote(total.at[j, half(other), :], out.at[:, cols(core, 2 * DH)], psend.at[j], precv.at[j], partner)
        keep = pltpu.make_async_copy(total.at[j, half(core), :], out.at[:, cols(core, 2 * DH)], lsem.at[2, 1 + j])
        now = [swap, keep]
        if j == 0:
            now += [
                remote(total.at[0], vx_out.at[k], xsend.at[k - 1], xrecv.at[k - 1], column_peer(k))
                for k in (1, 2, 3)
            ]
            now.append(pltpu.make_async_copy(total.at[0], vx_out.at[0], lsem.at[2, 3]))
        for copy in now:
            copy.start()
        tails += now
    for copy in tails + [dq_swap, dq_keep]:
        copy.wait()
    for j in (0, 1):
        for copy in sends[j]:
            copy.wait_send()

        @pl.when(has_prev)
        def _():
            aheads[j].wait_send()


def scatter(dq, dk, dv):
    dma = pltpu.SemaphoreType.DMA
    return pl.pallas_call(
        scatter_kernel,
        in_specs=[ANY] * 3,
        out_specs=[ANY] * 4,
        out_shape=[
            jax.ShapeDtypeStruct((T, 16 * DH), BF),
            jax.ShapeDtypeStruct((T, 4 * DH), BF),
            jax.ShapeDtypeStruct((T, 4 * DH), BF),
            jax.ShapeDtypeStruct((4, CHIP, 2 * DH), BF),
        ],
        scratch_shapes=[
            pltpu.VMEM((2, 3, CHIP, 2 * DH), BF),
            pltpu.VMEM((2, CHIP, 2 * DH), BF),
            pltpu.VMEM((2, 2, CHIP, 2 * DH), BF),
            pltpu.VMEM((2, CHIP, 2 * DH), BF),
            pltpu.VMEM((2, CHIP, 2 * DH), BF),
            dma((3, 4)), dma((3,)), dma((3,)), dma((2,)), dma((2,)),
            dma((2, 3)), dma((2, 3)), dma((3,)), dma((3,)),
        ],
        compiler_params=pltpu.CompilerParams(
            collective_id=1, has_side_effects=True, vmem_limit_bytes=32 << 20
        ),
        name="grad_scatter",
    )(dq, dk, dv)


def reduce_kernel(
    w_in, w_out, got, summed, far, rsend, rrecv, zsend, zrecv, lsem
):
    me = lax.axis_index("ctx")
    low = lax.axis_index("dp")
    core = lax.rem(me, 2)
    y = lax.rem(me // 2, 4)
    place = lax.rem(me, 32)
    z = (me // 32) * 4 + low
    row0 = me - 2 * y

    def row_peer(k):
        return row0 + 2 * lax.rem(y + k, 4)

    def z_peer(j, c):
        to = lax.rem(z + j, 8)
        return {"dp": lax.rem(to, 4), "ctx": (to // 4) * 32 + place - core + c}, to // 4

    barrier = pltpu.get_barrier_semaphore()
    for k in (1, 2, 3):
        signal(barrier, row_peer(k))
    for j in range(8):
        for i in (0, 1):
            if j or i:
                pl.semaphore_signal(
                    barrier,
                    inc=1,
                    device_id=z_peer(j, (core if i == 0 else 1 - core))[0],
                    device_id_type=MESH,
                )
    pl.semaphore_wait(barrier, 18)

    sends = [
        remote(w_in.at[:, lax.rem(y + k, 4)], got.at[k - 1], rsend.at[k - 1], rrecv.at[k - 1], row_peer(k))
        for k in (1, 2, 3)
    ]
    for copy in sends:
        copy.start()
    mine = pltpu.make_async_copy(w_in.at[:, y], got.at[3], lsem.at[0])
    mine.start()
    mine.wait()
    for copy in sends:
        copy.wait_recv()
    acc = got[3].astype(F32)
    for k in range(3):
        acc = acc + got[k].astype(F32)
    summed[...] = acc.astype(BF).reshape(2, 2, 64, 2 * DH)

    copies = []
    for j in range(8):
        for i in (0, 1):
            c = core if i == 0 else 1 - core
            peer, high = z_peer(j, c)
            src = summed.at[high, c]
            if j == 0 and i == 0:
                copies.append(pltpu.make_async_copy(src, far.at[0, 0], lsem.at[1]))
            else:
                copies.append(
                    pltpu.make_async_remote_copy(
                        src_ref=src,
                        dst_ref=far.at[i, j],
                        send_sem=zsend.at[i, j],
                        recv_sem=zrecv.at[i, j],
                        device_id=peer,
                        device_id_type=MESH,
                    )
                )
    for copy in copies:
        copy.start()
    for copy in copies:
        copy.wait()
    for copy in sends:
        copy.wait_send()
    same = far[0, 0].astype(F32)
    cross = far[1, 0].astype(F32)
    for j in range(1, 8):
        same = same + far[0, j].astype(F32)
        cross = cross + far[1, j].astype(F32)
    w_out[:, : 2 * DH] = jnp.where(core == 0, same, cross)
    w_out[:, 2 * DH :] = jnp.where(core == 0, cross, same)


def reduce_weight(part):
    dma = pltpu.SemaphoreType.DMA
    return pl.pallas_call(
        reduce_kernel,
        in_specs=[ANY],
        out_specs=VM,
        out_shape=jax.ShapeDtypeStruct((64, 4 * DH), F32),
        scratch_shapes=[
            pltpu.VMEM((4, 2, 128, 2 * DH), BF),
            pltpu.VMEM((2, 2, 64, 2 * DH), BF),
            pltpu.VMEM((2, 8, 64, 2 * DH), BF),
            dma((3,)), dma((3,)), dma((2, 8)), dma((2, 8)), dma((2,)),
        ],
        compiler_params=pltpu.CompilerParams(collective_id=2, has_side_effects=True),
        name="weight_reduce",
    )(part)


def gathered_inputs(rows):
    me = lax.axis_index("ctx")
    x = lax.rem(me // 8, 4)
    strips = rows.reshape(T, 2, 4, 512)

    def strip(k):
        return lax.dynamic_index_in_dim(strips, lax.rem(x + k, 4), 2, keepdims=False).reshape(T, 1024)

    def along(k):
        return [(i, i - (i // 8 % 4) * 8 + ((i // 8 + k) % 4) * 8) for i in range(64)]

    got = [strip(0)] + [lax.ppermute(strip(k), "ctx", along(k)) for k in (1, 2, 3)]
    mine = jnp.concatenate(got, axis=0)
    return mine, lax.ppermute(mine, "ctx", [(i, i ^ 1) for i in range(64)])


def on_device(
    inputs, value_weight, query_states, key_states, value_states, attention_out, out_grad, segment_ids
):
    core = lax.rem(lax.axis_index("ctx"), 2)
    weight = lax.all_gather(value_weight, "ctx", axis=0, tiled=True)
    x_mine, x_other = gathered_inputs(inputs[0])
    delta = jnp.sum(
        (out_grad[0].astype(F32) * attention_out[0].astype(F32)).reshape(T, 16, DH), axis=-1
    )
    delta = delta.T.reshape(2, 8, T)
    seg = jnp.broadcast_to(segment_ids, (8, T))
    q, do, de, kv, sg = gather(
        query_states[0], out_grad[0], delta, key_states[0], value_states[0], seg
    )
    ids = sg[:, :, 0, :]
    dq, dk, dv = attend(
        q, do, de, kv, ids[4], jnp.broadcast_to(ids.reshape(WIN, 1), (WIN, 128))
    )
    query_grad, key_grad, value_delta, value_rows = scatter(dq, dk, dv)
    value_rows = value_rows.reshape(4, 2, T, 2 * DH)
    v_mine = lax.dynamic_index_in_dim(value_rows, core, 1, keepdims=False).reshape(4 * T, 2 * DH)
    v_other = lax.dynamic_index_in_dim(value_rows, 1 - core, 1, keepdims=False).reshape(4 * T, 2 * DH)
    part = (dot(x_mine, v_mine, TN) + dot(x_other, v_other, TN)).astype(BF)
    weight_grad = reduce_weight(part.reshape(2, 4, 128, 2 * DH))
    input_grad = dot(value_delta, weight, NT).astype(BF)
    return (query_grad[None], key_grad[None], input_grad[None], weight_grad)


def solution(mesh):
    placed = (
        P("dp", "ctx", None),
        P("ctx", None),
        P("dp", "ctx", None),
        P("dp", "ctx", None),
        P("dp", "ctx", None),
        P("dp", "ctx", None),
        P("dp", "ctx", None),
        P("dp", "ctx"),
    )
    return jax.shard_map(
        on_device,
        mesh=mesh,
        in_specs=placed,
        out_specs=(
            P("dp", "ctx", None),
            P("dp", "ctx", None),
            P("dp", "ctx", None),
            P("ctx", None),
        ),
        check_vma=False,
    )
```

time: 1710 us -> 295 us (0.17)
  waiting for transfers between devices: 785 us -> 23.8 us
  loops' own time: 327 us -> 0 us
  local copies, waits for them, and re-layouts: 308 us -> 16 us
  Pallas kernels: 0 us -> 221 us
  matrix products: 126 us -> 8.75 us
  starting transfers between devices: 82 us -> 5.1 us
  other arithmetic: 33.3 us -> 2.58 us
  blocking collectives: 18.7 us -> 0 us
    unnamed x4 -> x1, waiting for transfers between devices: 470 us -> 0.68 us
    another operation x4 -> x0, loops' own time: 327 us -> none  [the longest x1 327 us: carried_in(): return lax.fori_loop(0, peers, turn, start)]
    dynamic_slice x348 -> x2, local copies, waits for them, and re-layouts: 231 us -> 0.22 us  [the longest x1 0.14 us: strip(): lax.dynamic_index_in_dim(strips, lax.rem(x + k, 4), 2, keepdims=False)]
    pallas_call x0 -> x4, Pallas kernels: none -> 221 us  [the longest x1 80.8 us: scatter(): pl.pallas_call(scatter_kernel, in_specs=[ANY] * 3, out_specs=[ANY] * 4, o...]
    ppermute x16 -> x4, waiting for transfers between devices: 157 us -> 23.1 us  [the longest x3 23.1 us: gathered_inputs(): lax.ppermute(strip(k), 'ctx', along(k))]
    all_gather x1, waiting for transfers between devices: 118 us -> 0.02 us  [on_device(): weight = lax.all_gather(value_weight, 'ctx', axis=0, tiled=True)]
    dot_general x18 -> x3, matrix products: 91.3 us -> 8.75 us  [dot(): return lax.dot_general(a, b, dims, preferred_element_type=F32)]
    ppermute x16 -> x4, starting transfers between devices: 81.9 us -> 5.06 us  [the longest x3 3.27 us: gathered_inputs(): lax.ppermute(strip(k), 'ctx', along(k))]
  transfers between devices with their start and end apart: 19 -> 5, of which waited for: 19 -> 3; matrix products, arithmetic and copies ran while one was open for 3% -> 6% of each run, Pallas kernels for 0% -> 76%
where the time goes in v1:
time: 295 us; the launch traced here: 291 us
  Pallas kernels  221 us (75%)
  waiting for transfers between devices  23.8 us (8%)
  local copies, waits for them, and re-layouts  16 us (5%)
  between operations  14.3 us (5%)
  matrix products  8.75 us (3%)
  starting transfers between devices  5.1 us (2%)
    pallas_call x1, Pallas kernels, scatter(): pl.pallas_call(scatter_kernel, in_specs=[ANY] * 3, out_specs=[ANY] * 4, o...  80.8 us
    pallas_call x1, Pallas kernels, attend(): pl.pallas_call(attend_kernel, grid=(2, 4, 2), in_specs=[heads, heads, pl....  60.4 us
    pallas_call x1, Pallas kernels, gather(): pl.pallas_call(gather_kernel, in_specs=[ANY] * 8, out_specs=[ANY] * 5, ou...  50.1 us
    pallas_call x1, Pallas kernels, reduce_weight(): pl.pallas_call(reduce_kernel, in_specs=[ANY], out_specs=VM, out_shape=jax...  29.7 us
    ppermute x3, waiting for transfers between devices, gathered_inputs(): lax.ppermute(strip(k), 'ctx', along(k))  23.1 us
    unnamed x31, local copies, waits for them, and re-layouts  9.2 us
    dot_general x3, matrix products, dot(): return lax.dot_general(a, b, dims, preferred_element_type=F32)  8.75 us
  transfers between devices with their start and end apart: 5, of which 3 were waited for; matrix products, arithmetic and copies ran while one was open for 6% of the time, Pallas kernels for 76%

profile of v1, /device:TPU:39, one launch (start us, length us, event | category | flops | bytes accessed | tf_op | source)
XLA Modules:
  0.0 291.4 jit_solution(1363805846328690438)
XLA Ops:
  7.2 0.0 all-gather.2.cloned.1.call-start
  7.2 0.7 all-gather.2.cloned.1.call-update
  8.0 3.3 %copy.18 = bf16[1,256,4096]{1,2,0:T(8,128)(2,1)S(1)} copy(bf16[1,256,4096]{2,1,0:T(8,128)(2,1)} %param.8) | data formatting | bytes 4194304 | tf_op args[0]
  11.3 0.1 constant_dynamic-slice_fusion.5
  11.4 0.6 collective-permute-start.2
  12.0 0.8 collective-permute-start.1
  12.9 1.8 collective-permute-start
  14.7 15.9 %collective-permute-done.2 = bf16[256,1024]{0,1:T(8,128)(2,1)S(1)} collective-permute-done((bf16[256,1024]{0,1:T(8,128)(2,1)S(1)}, bf16[256,1024]{0,1:T(8,128)(2,1)S(1)}, u32[]{:S(2)}, u32[]{:S(2)}) %collective-permute-start.2) | collective-permute-done | bytes 524320 | tf_op jit(solution)/shard_map/ppermute | solution.py:545
  30.6 0.0 copy-start.6
  30.6 5.2 %collective-permute-done.1 = bf16[256,1024]{0,1:T(8,128)(2,1)S(1)} collective-permute-done((bf16[256,1024]{0,1:T(8,128)(2,1)S(1)}, bf16[256,1024]{0,1:T(8,128)(2,1)S(1)}, u32[]{:S(2)}, u32[]{:S(2)}) %collective-permute-start.1) | collective-permute-done | bytes 524320 | tf_op jit(solution)/shard_map/ppermute | solution.py:545
  35.8 0.0 copy-start.8
  35.8 2.0 collective-permute-done
  37.8 0.0 copy-start.10
  37.8 0.0 copy-start.3
  37.8 0.0 copy-start.4
  37.8 1.6 pad_maximum_fusion
  39.4 0.0 copy-done.6
  39.4 0.0 copy-done.8
  39.4 0.0 copy-done.10
  39.4 1.8 collective-permute-start.3
  41.2 0.0 copy-done.3
  41.2 0.0 copy-done.4
  41.2 0.4 multiply_bitcast_fusion
  41.6 0.4 copy.19
  42.0 0.0 copy-start.12
  42.0 0.6 reduce_sum.9
  42.6 0.7 copy.16
  43.3 0.0 copy-done.12
  43.3 0.6 broadcast_in_dim.30.sg_in
  43.9 0.8 broadcast_in_dim.31.kv_zero
  44.7 0.6 broadcast_in_dim.32.sg_none
  45.3 50.1 %window_gather.1 = (bf16[512,1024]{1,0:T(8,128)(2,1)}, bf16[512,1024]{1,0:T(8,128)(2,1)}, f32[2,8,256]{2,1,0:T(8,128)}, bf16[2,2560,256]{2,1,0:T(8,128)(2,1)}, s32[5,2,8,256]{3,2,1,0:T(8,128)}) custom-call(bf16[256,2048]{1,0:T(8,128)(2,1)} %bitcast.41, bf16[256,2048]{1,0:T(8,128)(2,1)} %bitcast.38, f32[2,8,256]{2,1,0:T(8,128)} %bitcast.51, ...), custom_call_target="tpu_custom_call" | custom-call | tf_op jit(solution)/shard_map/window_gather/pallas_call | solution.py:169
  95.4 0.9 copy.17
  96.3 0.9 slice_reduce_fusion
  97.3 2.0 broadcast_in_dim.34.sk_ref
  99.2 0.0 copy-start
  99.2 1.2 copy-done
  100.5 0.0 copy-start.1
  100.5 1.2 copy-done.1
  101.7 0.0 copy-start.2
  101.7 0.7 copy-done.2
  102.4 60.4 %attend.1 = (bf16[512,1024]{1,0:T(8,128)(2,1)S(1)}, bf16[2560,256]{1,0:T(8,128)(2,1)S(1)}, bf16[2560,256]{1,0:T(8,128)(2,1)S(1)}) custom-call(bf16[512,1024]{1,0:T(8,128)(2,1)S(1)} %copy-done, bf16[512,1024]{1,0:T(8,128)(2,1)S(1)} %copy-done.1, f32[2,8,256]{2,1,0:T(8,128)S(1)} %copy-done.2, bf16[2,2560,256]{2,1,0:T(8,128)(2,1)} %get-tuple-element.19.k_ref.v_ref, ...), custom_call_target="tpu_custom_call" | custom-call | flops 12000000000 | bytes 9000000 | tf_op jit(solution)/shard_map/attend/pallas_call | solution.py:248
  162.8 80.8 %grad_scatter.1 = (bf16[256,2048]{1,0:T(8,128)(2,1)S(1)}, bf16[256,512]{1,0:T(8,128)(2,1)S(1)}, bf16[256,512]{1,0:T(8,128)(2,1)S(1)}, bf16[4,512,256]{2,1,0:T(8,128)(2,1)S(1)}) custom-call(bf16[512,1024]{1,0:T(8,128)(2,1)S(1)} %get-tuple-element.21.dq_in, bf16[2560,256]{1,0:T(8,128)(2,1)S(1)} %get-tuple-element.22.dk_in, ...), custom_call_target="tpu_custom_call" | custom-call | tf_op jit(solution)/shard_map/grad_scatter/pallas_call | solution.py:408
  243.5 0.1 constant_dynamic-slice_fusion.1
  243.6 0.0 collective-permute-done.3
  243.6 0.0 copy-start.7
  243.7 0.0 copy-start.9
  243.7 0.0 copy-start.11
  243.7 2.4 fusion.2
  246.1 0.0 copy-done.7
  246.1 0.0 copy-done.9
  246.1 0.0 copy-done.11
  246.1 1.5 fusion.1
  247.7 29.7 %weight_reduce.1 = f32[64,512]{1,0:T(8,128)} custom-call(bf16[2,4,128,256]{3,2,1,0:T(8,128)(2,1)} %bitcast.42), custom_call_target="tpu_custom_call" | custom-call | tf_op jit(solution)/shard_map/weight_reduce/pallas_call | solution.py:518
  277.4 0.0 all-gather.2.cloned.1.call-done
  277.4 4.8 %fusion = bf16[1,256,4096]{2,1,0:T(8,128)(2,1)} fusion(bf16[256,512]{1,0:T(8,128)(2,1)S(1)} %get-tuple-element.26, bf16[4096,512]{1,0:T(8,128)(2,1)} %all-gather.2.cloned.1.call-done), kind=kOutput, calls=%fused_computation.1 | convolution fusion | flops 1074790400 | bytes 6553600 | tf_op jit(solution)/shard_map/dot_general | solution.py:29
  282.2 0.0 copy-start.5
  282.2 1.0 copy.25
  283.2 0.7 copy.26
  283.9 0.0 copy-done.5
  283.9 0.7 copy.27
  (2 shorter events, 0.0 us)
Async XLA Ops:
  7.2 270.2 %all-gather.2.cloned.1.call-start = ((), (), s32[]{:S(2)}) async-start(), calls=%async_computation | async-start | bytes 4259840 | tf_op jit(solution)/shard_map/all_gather | solution.py:554
  11.4 19.2 %collective-permute-start.2 = (bf16[256,1024]{0,1:T(8,128)(2,1)S(1)}, bf16[256,1024]{0,1:T(8,128)(2,1)S(1)}, u32[]{:S(2)}, u32[]{:S(2)}) collective-permute-start(bf16[256,1024]{0,1:T(8,128)(2,1)S(1)} %bitcast.48), channel_id=1, source_target_pairs={{0,24},{1,25},{2,26},{3,27},{4,28},{5,29},{6,30},{7,31},{8,0},{9,1... | collective-permute-start | bytes 1572872 | tf_op jit(solution)/shard_map/ppermute | solution.py:545
  12.0 23.7 %collective-permute-start.1 = (bf16[256,1024]{0,1:T(8,128)(2,1)S(1)}, bf16[256,1024]{0,1:T(8,128)(2,1)S(1)}, u32[]{:S(2)}, u32[]{:S(2)}) collective-permute-start(bf16[256,1024]{0,1:T(8,128)(2,1)S(1)} %bitcast.47), channel_id=1, source_target_pairs={{0,16},{1,17},{2,18},{3,19},{4,20},{5,21},{6,22},{7,23},{8,24},{9,... | collective-permute-start | bytes 1572872 | tf_op jit(solution)/shard_map/ppermute | solution.py:545
  12.9 24.9 %collective-permute-start = (bf16[256,1024]{0,1:T(8,128)(2,1)S(1)}, bf16[256,1024]{0,1:T(8,128)(2,1)S(1)}, u32[]{:S(2)}, u32[]{:S(2)}) collective-permute-start(bf16[256,1024]{0,1:T(8,128)(2,1)S(1)} %bitcast.46), channel_id=1, source_target_pairs={{0,8},{1,9},{2,10},{3,11},{4,12},{5,13},{6,14},{7,15},{8,16},{9,17... | collective-permute-start | bytes 1572872 | tf_op jit(solution)/shard_map/ppermute | solution.py:545
  30.6 8.8 %copy-start.6 = (bf16[256,1024]{0,1:T(8,128)(2,1)}, bf16[256,1024]{0,1:T(8,128)(2,1)S(1)}, u32[]{:S(2)}) copy-start(bf16[256,1024]{0,1:T(8,128)(2,1)S(1)} %collective-permute-done.2) | copy-start | bytes 1572868
  35.8 3.6 %copy-start.8 = (bf16[256,1024]{0,1:T(8,128)(2,1)}, bf16[256,1024]{0,1:T(8,128)(2,1)S(1)}, u32[]{:S(2)}) copy-start(bf16[256,1024]{0,1:T(8,128)(2,1)S(1)} %collective-permute-done.1) | copy-start | bytes 1572868
  37.8 1.6 copy-start.10
  37.8 3.4 %copy-start.3 = (bf16[1,256,2048]{2,1,0:T(8,128)(2,1)S(1)}, bf16[1,256,2048]{2,1,0:T(8,128)(2,1)}, u32[]{:S(2)}) copy-start(bf16[1,256,2048]{2,1,0:T(8,128)(2,1)} %param.14) | copy-start | bytes 3145732
  37.8 3.4 %copy-start.4 = (bf16[1,256,2048]{2,1,0:T(8,128)(2,1)S(1)}, bf16[1,256,2048]{2,1,0:T(8,128)(2,1)}, u32[]{:S(2)}) copy-start(bf16[1,256,2048]{2,1,0:T(8,128)(2,1)} %param.13) | copy-start | bytes 3145732
  39.4 204.2 %collective-permute-start.3 = (bf16[1024,1024]{0,1:T(8,128)(2,1)}, bf16[1024,1024]{0,1:T(8,128)(2,1)}, u32[]{:S(2)}, u32[]{:S(2)}) collective-permute-start(bf16[1024,1024]{0,1:T(8,128)(2,1)} %pad_maximum_fusion), channel_id=1, source_target_pairs={{0,1},{1,0},{2,3},{3,2},{4,5},{5,4},{6,7},{7,6},{8,9},{9,8},{10,11... | collective-permute-start | bytes 6291464 | tf_op jit(solution)/shard_map/ppermute | solution.py:547
  42.0 1.3 copy-start.12
  99.2 1.2 copy-start
  100.5 1.2 copy-start.1
  101.7 0.7 copy-start.2
  243.6 2.5 copy-start.7
  243.7 2.5 copy-start.9
  243.7 2.5 copy-start.11
  282.2 1.7 copy-start.5
Sparse Core Ops, SparseCore 0:
  11.7 116.4 all-gather.1

commit v2 on v1

--- a/solution.py
+++ b/solution.py
@@ -190,9 +190,61 @@
 
 
 def attend_kernel(
-    q_ref, do_ref, de_ref, k_ref, v_ref, sq_ref, sk_ref, dq_ref, dk_ref, dv_ref, bias, s_ref, dk, dv
+    q_ref, do_ref, de_ref, k_ref, v_ref, sq_ref, sk_ref, x_in,
+    dq_ref, dk_ref, dv_ref, xg,
+    bias, s_ref, dk, dv, lsem, xsend, xrecv, fsend, frecv,
 ):
     g, h, t = pl.program_id(0), pl.program_id(1), pl.program_id(2)
+    step = (g * 4 + h) * 2 + t
+    me = lax.axis_index("ctx")
+    core = lax.rem(me, 2)
+    x = lax.rem(me // 8, 4)
+    partner = me + 1 - 2 * core
+
+    def column_peer(k):
+        return me - 8 * x + 8 * lax.rem(x + k, 4)
+
+    def strip(k, high):
+        start = pl.multiple_of(high * 2048 + lax.rem(x + k, 4) * 512, 512)
+        return x_in.at[:, pl.ds(start, 512)]
+
+    stays = [
+        pltpu.make_async_copy(strip(0, i), xg.at[core, 0, i], lsem.at[i]) for i in (0, 1)
+    ]
+    along = [
+        remote(strip(k, i), xg.at[core, k, i], xsend.at[k - 1, i], xrecv.at[k - 1, i], column_peer(k))
+        for k in (1, 2, 3)
+        for i in (0, 1)
+    ]
+    forward = [
+        remote(xg.at[core, k], xg.at[core, k], fsend.at[k], frecv.at[k], partner) for k in range(4)
+    ]
+
+    @pl.when(step == 0)
+    def _():
+        barrier = pltpu.get_barrier_semaphore()
+        signal(barrier, partner)
+        for k in (1, 2, 3):
+            signal(barrier, column_peer(k))
+        pl.semaphore_wait(barrier, 4)
+        for copy in stays + along:
+            copy.start()
+
+    @pl.when(step == 11)
+    def _():
+        for copy in stays:
+            copy.wait()
+        for copy in along:
+            copy.wait_recv()
+        for copy in forward:
+            copy.start()
+
+    @pl.when(step == 15)
+    def _():
+        for copy in along:
+            copy.wait_send()
+        for copy in forward:
+            copy.wait()
 
     def rows(c):
         return pl.ds(pl.multiple_of(t * T + c * T, T), T)
@@ -242,7 +294,8 @@
         dv_ref[...] = dv[...].astype(BF)
 
 
-def attend(q, do, de, kv, sq, sk):
+def attend(q, do, de, kv, sq, sk, x):
+    dma = pltpu.SemaphoreType.DMA
     heads = pl.BlockSpec((T, DH), lambda g, h, t: (t, g * 4 + h))
     window = pl.BlockSpec((WIN, DH), lambda g, h, t: (0, g))
     return pl.pallas_call(
@@ -256,25 +309,30 @@
             pl.BlockSpec((1, WIN, DH), lambda g, h, t: (1, 0, g)),
             pl.BlockSpec((2, T), lambda g, h, t: (0, 0)),
             pl.BlockSpec((WIN, 128), lambda g, h, t: (0, 0)),
-        ],
-        out_specs=[heads, window, window],
+            ANY,
+        ],
+        out_specs=[heads, window, window, ANY],
         out_shape=[
             jax.ShapeDtypeStruct((CHIP, 8 * DH), BF),
             jax.ShapeDtypeStruct((WIN, 2 * DH), BF),
             jax.ShapeDtypeStruct((WIN, 2 * DH), BF),
+            jax.ShapeDtypeStruct((2, 4, 2, T, 512), BF),
         ],
         scratch_shapes=[
             pltpu.VMEM((2, NK, T, T), F32),
             pltpu.VMEM((NK, T, T), F32),
             pltpu.VMEM((WIN, DH), F32),
             pltpu.VMEM((WIN, DH), F32),
-        ],
-        compiler_params=pltpu.CompilerParams(vmem_limit_bytes=48 << 20),
+            dma((2,)), dma((3, 2)), dma((3, 2)), dma((4,)), dma((4,)),
+        ],
+        compiler_params=pltpu.CompilerParams(
+            collective_id=3, has_side_effects=True, vmem_limit_bytes=40 << 20
+        ),
         cost_estimate=pl.CostEstimate(
             flops=12_000_000_000, bytes_accessed=9_000_000, transcendentals=9_400_000
         ),
         name="attend",
-    )(q, do, de, kv, kv, sq, sk)
+    )(q, do, de, kv, kv, sq, sk, x)
 
 
 def scatter_kernel(
@@ -378,17 +436,17 @@
         def _():
             ahead_buf[j] = jnp.zeros_like(ahead_buf[j])
 
-        total[j] = (mine + ahead_buf[j].astype(F32)).astype(BF)
+        total[j] = (mine + ahead_buf[j].astype(F32)).astype(BF).reshape(2, T, 2 * DH)
         out = (vd_out, dk_out)[j]
-        swap = remote(total.at[j, half(other), :], out.at[:, cols(core, 2 * DH)], psend.at[j], precv.at[j], partner)
-        keep = pltpu.make_async_copy(total.at[j, half(core), :], out.at[:, cols(core, 2 * DH)], lsem.at[2, 1 + j])
+        swap = remote(total.at[j, other], out.at[:, cols(core, 2 * DH)], psend.at[j], precv.at[j], partner)
+        keep = pltpu.make_async_copy(total.at[j, core], out.at[:, cols(core, 2 * DH)], lsem.at[2, 1 + j])
         now = [swap, keep]
         if j == 0:
             now += [
-                remote(total.at[0], vx_out.at[k], xsend.at[k - 1], xrecv.at[k - 1], column_peer(k))
+                remote(total.at[0], vx_out.at[:, k], xsend.at[k - 1], xrecv.at[k - 1], column_peer(k))
                 for k in (1, 2, 3)
             ]
-            now.append(pltpu.make_async_copy(total.at[0], vx_out.at[0], lsem.at[2, 3]))
+            now.append(pltpu.make_async_copy(total.at[0], vx_out.at[:, 0], lsem.at[2, 3]))
         for copy in now:
             copy.start()
         tails += now
@@ -413,14 +471,14 @@
             jax.ShapeDtypeStruct((T, 16 * DH), BF),
             jax.ShapeDtypeStruct((T, 4 * DH), BF),
             jax.ShapeDtypeStruct((T, 4 * DH), BF),
-            jax.ShapeDtypeStruct((4, CHIP, 2 * DH), BF),
+            jax.ShapeDtypeStruct((2, 4, T, 2 * DH), BF),
         ],
         scratch_shapes=[
             pltpu.VMEM((2, 3, CHIP, 2 * DH), BF),
             pltpu.VMEM((2, CHIP, 2 * DH), BF),
             pltpu.VMEM((2, 2, CHIP, 2 * DH), BF),
             pltpu.VMEM((2, CHIP, 2 * DH), BF),
-            pltpu.VMEM((2, CHIP, 2 * DH), BF),
+            pltpu.VMEM((2, 2, T, 2 * DH), BF),
             dma((3, 4)), dma((3,)), dma((3,)), dma((2,)), dma((2,)),
             dma((2, 3)), dma((2, 3)), dma((3,)), dma((3,)),
         ],
@@ -432,7 +490,7 @@
 
 
 def reduce_kernel(
-    w_in, w_out, got, summed, far, rsend, rrecv, zsend, zrecv, lsem
+    xg, vx, vd, weight, w_out, in_out, part, got, summed, far, rsend, rrecv, zsend, zrecv, lsem
 ):
     me = lax.axis_index("ctx")
     low = lax.axis_index("dp")
@@ -463,18 +521,26 @@
                 )
     pl.semaphore_wait(barrier, 18)
 
+    for i in (0, 1):
+        acc = jnp.zeros((512, 2 * DH), F32)
+        for a in (0, 1):
+            for k in range(4):
+                acc = acc + dot(xg[a, k, i], vx[a, k], TN)
+        part[i] = acc.astype(BF).reshape(4, 128, 2 * DH)
+
     sends = [
-        remote(w_in.at[:, lax.rem(y + k, 4)], got.at[k - 1], rsend.at[k - 1], rrecv.at[k - 1], row_peer(k))
+        remote(part.at[:, lax.rem(y + k, 4)], got.at[k - 1], rsend.at[k - 1], rrecv.at[k - 1], row_peer(k))
         for k in (1, 2, 3)
     ]
     for copy in sends:
         copy.start()
-    mine = pltpu.make_async_copy(w_in.at[:, y], got.at[3], lsem.at[0])
-    mine.start()
-    mine.wait()
+    for i in range(8):
+        in_out[:, i * 512 : (i + 1) * 512] = dot(
+            vd[...], weight[i * 512 : (i + 1) * 512, :], NT
+        ).astype(BF)
     for copy in sends:
         copy.wait_recv()
-    acc = got[3].astype(F32)
+    acc = part[:, y].astype(F32)
     for k in range(3):
         acc = acc + got[k].astype(F32)
     summed[...] = acc.astype(BF).reshape(2, 2, 64, 2 * DH)
@@ -486,7 +552,7 @@
             peer, high = z_peer(j, c)
             src = summed.at[high, c]
             if j == 0 and i == 0:
-                copies.append(pltpu.make_async_copy(src, far.at[0, 0], lsem.at[1]))
+                copies.append(pltpu.make_async_copy(src, far.at[0, 0], lsem))
             else:
                 copies.append(
                     pltpu.make_async_remote_copy(
@@ -513,46 +579,34 @@
     w_out[:, 2 * DH :] = jnp.where(core == 0, cross, same)
 
 
-def reduce_weight(part):
+def reduce_weight(xg, vx, vd, weight):
     dma = pltpu.SemaphoreType.DMA
     return pl.pallas_call(
         reduce_kernel,
-        in_specs=[ANY],
-        out_specs=VM,
-        out_shape=jax.ShapeDtypeStruct((64, 4 * DH), F32),
+        in_specs=[VM] * 4,
+        out_specs=[VM, VM],
+        out_shape=[
+            jax.ShapeDtypeStruct((64, 4 * DH), F32),
+            jax.ShapeDtypeStruct((T, 4096), BF),
+        ],
         scratch_shapes=[
-            pltpu.VMEM((4, 2, 128, 2 * DH), BF),
+            pltpu.VMEM((2, 4, 128, 2 * DH), BF),
+            pltpu.VMEM((3, 2, 128, 2 * DH), BF),
             pltpu.VMEM((2, 2, 64, 2 * DH), BF),
             pltpu.VMEM((2, 8, 64, 2 * DH), BF),
-            dma((3,)), dma((3,)), dma((2, 8)), dma((2, 8)), dma((2,)),
-        ],
-        compiler_params=pltpu.CompilerParams(collective_id=2, has_side_effects=True),
+            dma((3,)), dma((3,)), dma((2, 8)), dma((2, 8)), dma,
+        ],
+        compiler_params=pltpu.CompilerParams(
+            collective_id=2, has_side_effects=True, vmem_limit_bytes=32 << 20
+        ),
         name="weight_reduce",
-    )(part)
-
-
-def gathered_inputs(rows):
-    me = lax.axis_index("ctx")
-    x = lax.rem(me // 8, 4)
-    strips = rows.reshape(T, 2, 4, 512)
-
-    def strip(k):
-        return lax.dynamic_index_in_dim(strips, lax.rem(x + k, 4), 2, keepdims=False).reshape(T, 1024)
-
-    def along(k):
-        return [(i, i - (i // 8 % 4) * 8 + ((i // 8 + k) % 4) * 8) for i in range(64)]
-
-    got = [strip(0)] + [lax.ppermute(strip(k), "ctx", along(k)) for k in (1, 2, 3)]
-    mine = jnp.concatenate(got, axis=0)
-    return mine, lax.ppermute(mine, "ctx", [(i, i ^ 1) for i in range(64)])
+    )(xg, vx, vd, weight)
 
 
 def on_device(
     inputs, value_weight, query_states, key_states, value_states, attention_out, out_grad, segment_ids
 ):
-    core = lax.rem(lax.axis_index("ctx"), 2)
     weight = lax.all_gather(value_weight, "ctx", axis=0, tiled=True)
-    x_mine, x_other = gathered_inputs(inputs[0])
     delta = jnp.sum(
         (out_grad[0].astype(F32) * attention_out[0].astype(F32)).reshape(T, 16, DH), axis=-1
     )
@@ -562,16 +616,11 @@
         query_states[0], out_grad[0], delta, key_states[0], value_states[0], seg
     )
     ids = sg[:, :, 0, :]
-    dq, dk, dv = attend(
-        q, do, de, kv, ids[4], jnp.broadcast_to(ids.reshape(WIN, 1), (WIN, 128))
+    dq, dk, dv, xg = attend(
+        q, do, de, kv, ids[4], jnp.broadcast_to(ids.reshape(WIN, 1), (WIN, 128)), inputs[0]
     )
     query_grad, key_grad, value_delta, value_rows = scatter(dq, dk, dv)
-    value_rows = value_rows.reshape(4, 2, T, 2 * DH)
-    v_mine = lax.dynamic_index_in_dim(value_rows, core, 1, keepdims=False).reshape(4 * T, 2 * DH)
-    v_other = lax.dynamic_index_in_dim(value_rows, 1 - core, 1, keepdims=False).reshape(4 * T, 2 * DH)
-    part = (dot(x_mine, v_mine, TN) + dot(x_other, v_other, TN)).astype(BF)
-    weight_grad = reduce_weight(part.reshape(2, 4, 128, 2 * DH))
-    input_grad = dot(value_delta, weight, NT).astype(BF)
+    weight_grad, input_grad = reduce_weight(xg, value_rows, value_delta, weight)
     return (query_grad[None], key_grad[None], input_grad[None], weight_grad)
 
 

time: 295 us -> 262 us (0.89)
  waiting for transfers between devices: 23.8 us -> 0.7 us
  matrix products: 8.75 us -> 0 us
  starting transfers between devices: 5.1 us -> 0.04 us
    pallas_call x1, Pallas kernels: 60.4 us -> 99.9 us  [attend(): pl.pallas_call(attend_kernel, grid=(2, 4, 2), in_specs=[heads, heads, pl....]
    pallas_call x1, Pallas kernels: 80.8 us -> 45.8 us  [scatter(): pl.pallas_call(scatter_kernel, in_specs=[ANY] * 3, out_specs=[ANY] * 4, o...]
    ppermute x4 -> x0, waiting for transfers between devices: 23.1 us -> none  [the longest x3 23.1 us: gathered_inputs(): lax.ppermute(strip(k), 'ctx', along(k))]
    dot_general x3 -> x0, matrix products: 8.75 us -> none  [dot(): return lax.dot_general(a, b, dims, preferred_element_type=F32)]
    ppermute x4 -> x0, starting transfers between devices: 5.06 us -> none  [the longest x3 3.27 us: gathered_inputs(): lax.ppermute(strip(k), 'ctx', along(k))]
    unnamed x31 -> x21, local copies, waits for them, and re-layouts: 9.2 us -> 13.4 us
  transfers between devices with their start and end apart: 5 -> 1, of which waited for: 3 -> 0; matrix products, arithmetic and copies ran while one was open for 6% -> 3% of each run, Pallas kernels for 76% -> 76%
where the time goes in v2:
time: 262 us; the launch traced here: 258 us
  Pallas kernels  222 us (85%)
  local copies, waits for them, and re-layouts  18.4 us (7%)
  between operations  14.2 us (5%)
    pallas_call x1, Pallas kernels, attend(): pl.pallas_call(attend_kernel, grid=(2, 4, 2), in_specs=[heads, heads, pl....  99.9 us
    pallas_call x1, Pallas kernels, gather(): pl.pallas_call(gather_kernel, in_specs=[ANY] * 8, out_specs=[ANY] * 5, ou...  49.4 us
    pallas_call x1, Pallas kernels, scatter(): pl.pallas_call(scatter_kernel, in_specs=[ANY] * 3, out_specs=[ANY] * 4, o...  45.8 us
    pallas_call x1, Pallas kernels, reduce_weight(): pl.pallas_call(reduce_kernel, in_specs=[VM] * 4, out_specs=[VM, VM], out_...  27.1 us
    unnamed x21, local copies, waits for them, and re-layouts  13.4 us
  transfers between devices with their start and end apart: 1, of which 0 were waited for; matrix products, arithmetic and copies ran while one was open for 3% of the time, Pallas kernels for 76%

profile of v2, /device:TPU:39, one launch (start us, length us, event | category | flops | bytes accessed | tf_op | source)
XLA Modules:
  0.0 257.9 jit_solution(1094877130791457009)
XLA Ops:
  7.2 0.0 all-gather.2.cloned.1.call-start
  7.2 0.7 all-gather.2.cloned.1.call-update
  7.9 1.9 multiply_bitcast_fusion
  9.8 0.4 copy.15
  10.2 0.0 copy-start.7
  10.2 0.6 reduce_sum.9
  10.8 0.7 copy.13
  11.5 0.0 copy-done.7
  11.5 0.6 broadcast_in_dim.30.sg_in
  12.1 0.8 broadcast_in_dim.31.kv_zero
  12.9 0.6 broadcast_in_dim.32.sg_none
  13.5 0.0 copy-start.3
  13.5 49.4 %window_gather.1 = (bf16[512,1024]{1,0:T(8,128)(2,1)}, bf16[512,1024]{1,0:T(8,128)(2,1)}, f32[2,8,256]{2,1,0:T(8,128)}, bf16[2,2560,256]{2,1,0:T(8,128)(2,1)}, s32[5,2,8,256]{3,2,1,0:T(8,128)}) custom-call(bf16[256,2048]{1,0:T(8,128)(2,1)} %bitcast.25, bf16[256,2048]{1,0:T(8,128)(2,1)} %bitcast.24, f32[2,8,256]{2,1,0:T(8,128)} %bitcast.29, ...), custom_call_target="tpu_custom_call" | custom-call | tf_op jit(solution)/shard_map/window_gather/pallas_call | solution.py:169
  62.9 0.9 copy.14
  63.9 0.9 slice_reduce_fusion
  64.8 0.4 broadcast_in_dim.34.sk_ref
  65.2 0.0 copy-done.3
  65.2 0.0 copy-start.2
  65.2 1.7 copy-done.2
  67.0 0.0 copy-start.4
  67.0 1.3 copy-done.4
  68.3 0.0 copy-start.5
  68.3 1.2 copy-done.5
  69.5 0.0 copy-start.6
  69.5 0.7 copy-done.6
  70.2 99.9 %attend.1 = (bf16[512,1024]{1,0:T(8,128)(2,1)S(1)}, bf16[2560,256]{1,0:T(8,128)(2,1)S(1)}, bf16[2560,256]{1,0:T(8,128)(2,1)S(1)}, bf16[2,4,2,256,512]{4,3,2,1,0:T(8,128)(2,1)}) custom-call(bf16[512,1024]{1,0:T(8,128)(2,1)S(1)} %copy-done.4, bf16[512,1024]{1,0:T(8,128)(2,1)S(1)} %copy-done.5, f32[2,8,256]{2,1,0:T(8,128)S(1)} %copy-done.6, ...), custom_call_target="tpu_custom_call" | custom-call | flops 12000000000 | bytes 9000000 | tf_op jit(solution)/shard_map/attend/pallas_call | solution.py:301
  170.1 45.8 %grad_scatter.1 = (bf16[256,2048]{1,0:T(8,128)(2,1)S(1)}, bf16[256,512]{1,0:T(8,128)(2,1)S(1)}, bf16[256,512]{1,0:T(8,128)(2,1)S(1)}, bf16[2,4,256,256]{3,2,1,0:T(8,128)(2,1)S(1)}) custom-call(bf16[512,1024]{1,0:T(8,128)(2,1)S(1)} %get-tuple-element.24.dq_in, bf16[2560,256]{1,0:T(8,128)(2,1)S(1)} %get-tuple-element.25.dk_in, ...), custom_call_target="tpu_custom_call" | custom-call | tf_op jit(solution)/shard_map/grad_scatter/pallas_call | solution.py:466
  215.9 0.0 all-gather.2.cloned.1.call-done.weight
  215.9 0.0 copy-start
  216.0 2.2 copy-done
  218.1 0.0 copy-start.1
  218.1 2.2 copy-done.1
  220.3 27.1 %weight_reduce.1 = (f32[64,512]{1,0:T(8,128)S(1)}, bf16[256,4096]{1,0:T(8,128)(2,1)S(1)}) custom-call(bf16[2,4,2,256,512]{4,3,2,1,0:T(8,128)(2,1)S(1)} %copy-done.1, bf16[2,4,256,256]{3,2,1,0:T(8,128)(2,1)S(1)} %get-tuple-element.30.vx, bf16[256,512]{1,0:T(8,128)(2,1)S(1)} %get-tuple-element.31.vd, bf16[4096,512]{1,0:T(8,128)(2,1)S(1)} %copy-done), custom_call_target="tpu_custom_call" | custom-call | tf_op jit(solution)/shard_map/weight_reduce/pallas_call | solution.py:584
  247.4 1.0 copy.22
  248.4 0.7 copy.23
  249.1 1.3 copy.24
  250.4 0.7 copy.25
  (2 shorter events, 0.0 us)
Async XLA Ops:
  7.2 208.8 %all-gather.2.cloned.1.call-start = ((), (), s32[]{:S(2)}) async-start(), calls=%async_computation | async-start | bytes 4259840 | tf_op jit(solution)/shard_map/all_gather | solution.py:609
  10.2 1.3 copy-start.7
  13.5 51.7 %copy-start.3 = (bf16[1,256,4096]{2,1,0:T(8,128)(2,1)S(1)}, bf16[1,256,4096]{2,1,0:T(8,128)(2,1)}, u32[]{:S(2)}) copy-start(bf16[1,256,4096]{2,1,0:T(8,128)(2,1)} %param.8) | copy-start | bytes 6291460
  65.2 1.7 copy-start.2
  67.0 1.3 copy-start.4
  68.3 1.2 copy-start.5
  69.5 0.7 copy-start.6
  215.9 2.2 copy-start
  218.1 2.2 copy-start.1
Sparse Core Ops, SparseCore 0:
  11.7 119.5 all-gather.1

commit v3 on v0

v3 whole, which is shorter than its diff:
```python
import math

import jax
import jax.numpy as jnp
from jax import lax
from jax.experimental import pallas as pl
from jax.experimental.pallas import tpu as pltpu
from jax.sharding import PartitionSpec as P

DH = 128
W = 2048
T = 256
CHIP = 2 * T
NK = W // T + 1
WIN = W + CHIP
FACTOR = 1.0 / math.sqrt(DH)
FACTOR2 = FACTOR * math.log2(math.e)
BF = jnp.bfloat16
F32 = jnp.float32
MESH = pl.DeviceIdType.MESH
ANY = pl.BlockSpec(memory_space=pl.ANY)
VM = pl.BlockSpec(memory_space=pltpu.VMEM)
NT = (((1,), (1,)), ((), ()))
NN = (((1,), (0,)), ((), ()))
TN = (((0,), (0,)), ((), ()))


def dot(a, b, dims):
    return lax.dot_general(a, b, dims, preferred_element_type=F32)


def signal(sem, ctx):
    pl.semaphore_signal(sem, inc=1, device_id={"ctx": ctx}, device_id_type=MESH)


def remote(src, dst, send, recv, ctx):
    return pltpu.make_async_remote_copy(
        src_ref=src,
        dst_ref=dst,
        send_sem=send,
        recv_sem=recv,
        device_id={"ctx": ctx},
        device_id_type=MESH,
    )


def main_kernel(
    q_in, do_in, o_in, k_in, v_in, sg_in, x_in,
    dq_out, vd_out, vx_out, dk_out, xg,
    q_s, do_s, o_s, kv, sg, bias, s_ref, p_ref, acc, dq_s, dvp, dkp, got, part, ahead, total,
    lsem, psend, precv, asend, arecv, rsend, rrecv, gsend, grecv, hsend, hrecv,
    vsend, vrecv, xsend, xrecv, fsend, frecv,
):
    me = lax.axis_index("ctx")
    core = lax.rem(me, 2)
    other = 1 - core
    y = lax.rem(me // 2, 4)
    x = lax.rem(me // 8, 4)
    partner = me + 1 - 2 * core
    has_next = me < 56
    has_prev = me >= 8
    far_next = (x == 3) & has_next
    far_prev = (x == 0) & has_prev

    def row_peer(k):
        return me - 2 * y + 2 * lax.rem(y + k, 4)

    def column_peer(k):
        return me - 8 * x + 8 * lax.rem(x + k, 4)

    barrier = pltpu.get_barrier_semaphore()
    signal(barrier, partner)
    for k in (1, 2, 3):
        signal(barrier, row_peer(k))
        signal(barrier, column_peer(k))

    @pl.when(far_next)
    def _():
        signal(barrier, me + 8)

    @pl.when(far_prev)
    def _():
        signal(barrier, me - 8)

    sg[4, core] = jnp.broadcast_to(sg_in[...], (8, T))

    @pl.when(jnp.logical_not(has_prev))
    def _():
        kv[:, :CHIP, :] = jnp.zeros((4, CHIP, DH), BF)
        sg[0] = jnp.full((2, 8, T), -1, jnp.int32)

    pl.semaphore_wait(barrier, 7 + far_next.astype(jnp.int32) + far_prev.astype(jnp.int32))

    half = pl.ds(pl.multiple_of(core * T, T), T)
    rest = pl.ds(pl.multiple_of(other * T, T), T)
    home = pl.ds(pl.multiple_of(W + core * T, T), T)

    def cols(start, n):
        return pl.ds(pl.multiple_of(start * n, n), n)

    def source(i, c):
        if i < 4:
            return (k_in, v_in)[i // 2].at[:, cols(c * 2 + i % 2, DH)]
        return (q_in, do_in, o_in)[i - 4].at[:, cols(c, 8 * DH)]

    def target(i):
        if i < 4:
            return kv.at[i, home, :]
        return (q_s, do_s, o_s)[i - 4].at[half, :]

    swaps = [remote(source(i, other), target(i), psend.at[i], precv.at[i], partner) for i in range(7)]
    stays = [pltpu.make_async_copy(source(i, core), target(i), lsem.at[i]) for i in range(7)]
    sg_swap = remote(sg.at[4, core], sg.at[4, core], psend.at[7], precv.at[7], partner)

    def both(i):
        stays[i].start()
        swaps[i].start()

    both(0)
    sg_swap.start()
    for i in (4, 5, 1, 2, 3, 6):
        both(i)

    def block(u, s):
        if u == 4:
            return sg.at[s]
        return kv.at[u, pl.ds(s * CHIP, CHIP), :]

    def forth(u):
        return remote(block(u, 4), block(u, 0), asend.at[u], arecv.at[u], me + 8)

    def along(u, k, s):
        return remote(
            block(u, s), block(u, 4 - k), rsend.at[u, k - 1], rrecv.at[u, k - 1], row_peer(k)
        )

    def send_own(u):
        if u == 4:
            sg_swap.wait_recv()
        else:
            stays[u].wait()
            swaps[u].wait_recv()

        @pl.when(has_next)
        def _():
            forth(u).start()

        for k in (1, 2, 3):

            @pl.when(y + k < 4)
            def _():
                along(u, k, 4).start()

    def relay(u):
        @pl.when(has_prev)
        def _():
            forth(u).wait_recv()

        for k in (1, 2, 3):

            @pl.when(y + k >= 4)
            def _():
                along(u, k, 0).start()

    def arrived(u):
        for k in (1, 2, 3):
            along(u, k, 4).wait_recv()

    send_own(4)
    send_own(0)
    relay(4)
    relay(0)
    for i in (4, 5):
        stays[i].wait()
        swaps[i].wait_recv()
    arrived(4)

    for i in range(NK + 1):
        sk = jnp.transpose(sg[i // 2, i % 2].astype(F32))[:, :1]
        sk = jnp.broadcast_to(sk, (T, T))
        for t in (0, 1):
            c = i - t
            if 0 <= c < NK:
                live = sk == sg[4, t][:1, :].astype(F32)
                kpos = lax.broadcasted_iota(jnp.int32, (T, T), 0)
                qpos = lax.broadcasted_iota(jnp.int32, (T, T), 1)
                if c == 0:
                    live = live & (kpos > qpos)
                if c == NK - 1:
                    live = live & (kpos <= qpos)
                bias[t, c] = jnp.where(live, 0.0, -1e30)
    arrived(0)

    def give(g, k):
        return remote(
            dvp.at[g, pl.ds((4 - k) * CHIP, CHIP), :],
            got.at[g, k - 1],
            gsend.at[g, k - 1],
            grecv.at[g, k - 1],
            row_peer(4 - k),
        )

    def back(g):
        return remote(part.at[g], ahead.at[g], hsend.at[g], hrecv.at[g], me - 8)

    def give_start(g):
        for k in (1, 2, 3):
            give(g, k).start()

    def give_sum(g):
        for k in (1, 2, 3):
            give(g, k).wait_recv()
        before = dvp[g, :CHIP, :].astype(F32)
        for k in (1, 2, 3):
            before = before + jnp.where(y + k >= 4, got[g, k - 1].astype(F32), 0.0)
        part[g] = before.astype(BF)

        @pl.when(has_prev)
        def _():
            back(g).start()

    def spread(g):
        return [
            remote(
                total.at[g],
                vx_out.at[:, k, :, pl.ds(g * DH, DH)],
                vsend.at[g, k - 1],
                vrecv.at[g, k - 1],
                column_peer(k),
            )
            for k in (1, 2, 3)
        ] + [
            remote(
                total.at[g, other],
                vd_out.at[:, cols(core * 2 + g, DH)],
                psend.at[8 + g],
                precv.at[8 + g],
                partner,
            )
        ]

    def keep(g):
        return [
            pltpu.make_async_copy(total.at[g], vx_out.at[:, 0, :, pl.ds(g * DH, DH)], lsem.at[8 + g]),
            pltpu.make_async_copy(
                total.at[g, core], vd_out.at[:, cols(core * 2 + g, DH)], lsem.at[10 + g]
            ),
        ]

    def give_total(g):
        @pl.when(has_next)
        def _():
            back(g).wait_recv()

        @pl.when(jnp.logical_not(has_next))
        def _():
            ahead[g] = jnp.zeros((CHIP, DH), BF)

        mine = dvp[g, W:, :].astype(F32) + ahead[g].astype(F32)
        for k in (1, 2, 3):
            mine = mine + jnp.where(y + k < 4, got[g, k - 1].astype(F32), 0.0)
        total[g] = mine.astype(BF).reshape(2, T, DH)
        for copy in spread(g) + keep(g):
            copy.start()

    def strip(k, high):
        start = pl.multiple_of(high * 2048 + lax.rem(x + k, 4) * 512, 512)
        return x_in.at[:, pl.ds(start, 512)]

    def x_keep():
        return [pltpu.make_async_copy(strip(0, i), xg.at[core, 0, i], lsem.at[12 + i]) for i in (0, 1)]

    def x_along():
        return [
            remote(
                strip(k, i), xg.at[core, k, i], xsend.at[k - 1, i], xrecv.at[k - 1, i], column_peer(k)
            )
            for k in (1, 2, 3)
            for i in (0, 1)
        ]

    def x_forward():
        return [
            remote(xg.at[core, k], xg.at[core, k], fsend.at[k], frecv.at[k], partner) for k in range(4)
        ]

    def at(n, when, *calls):
        @pl.when(n == when)
        def _():
            for f, *args in calls:
                f(*args)

    def start_all(make):
        for copy in make():
            copy.start()

    def x_pass():
        for copy in x_keep():
            copy.wait()
        for copy in x_along():
            copy.wait_recv()
        for copy in x_forward():
            copy.start()

    def rows(t, c):
        return pl.ds(pl.multiple_of(t * T + c * T, T), T)

    def phase1(n, _):
        g, h, t = n // 8, lax.rem(n // 2, 4), lax.rem(n, 2)
        at(n, 0, (send_own, 1))
        at(n, 3, (relay, 1), (send_own, 2))
        at(n, 8, (arrived, 1), (relay, 2), (send_own, 3), (give_start, 0))
        at(n, 12, (relay, 3), (start_all, x_keep), (start_all, x_along))

        @pl.when(lax.rem(n, 8) == 0)
        def _():
            acc[...] = jnp.zeros_like(acc)

        head = pl.ds(pl.multiple_of((g * 4 + h) * DH, DH), DH)
        here = pl.ds(pl.multiple_of(t * T, T), T)
        q, do = q_s[here, head], do_s[here, head]
        top = jnp.full((8, T), -1e30, F32)
        for c in range(NK):
            s = dot(kv[g, rows(t, c), :], q, NT) + bias[t, c]
            s_ref[c] = s
            top = jnp.maximum(top, jnp.max(s.reshape(T // 8, 8, T), axis=0))
        top = jnp.max(top, axis=0, keepdims=True)
        weight = jnp.zeros((8, T), F32)
        for c in range(NK):
            e = jnp.exp2((s_ref[c] - top) * FACTOR2)
            s_ref[c] = e
            weight = weight + jnp.sum(e.reshape(T // 8, 8, T), axis=0)
        inverse = 1.0 / jnp.sum(weight, axis=0, keepdims=True)
        for c in range(NK):
            p = (s_ref[c] * inverse).astype(BF)
            p_ref[n, c] = p
            acc[rows(t, c), :] += dot(p, do, NN)

        @pl.when(lax.rem(n, 8) == 7)
        def _():
            dvp[g] = acc[...].astype(BF)

        return 0

    lax.fori_loop(0, 16, phase1, 0)

    def dq_swap(g):
        block = pl.ds(g * 4 * DH, 4 * DH)
        place = cols(core * 2 + g, 4 * DH)
        return [
            remote(dq_s.at[rest, block], dq_out.at[:, place], psend.at[10 + g], precv.at[10 + g], partner),
            pltpu.make_async_copy(dq_s.at[half, block], dq_out.at[:, place], lsem.at[14 + g]),
        ]

    stays[6].wait()
    swaps[6].wait_recv()
    give_start(1)
    arrived(2)

    def phase2(n, _):
        g, h, t = n // 8, lax.rem(n // 2, 4), lax.rem(n, 2)
        at(n, 1, (give_sum, 0))
        at(n, 4, (give_total, 0), (give_sum, 1))
        at(n, 6, (x_pass,))
        at(n, 8, (arrived, 3), (start_all, lambda: dq_swap(0)))
        at(n, 10, (give_total, 1))

        @pl.when(lax.rem(n, 8) == 0)
        def _():
            acc[...] = jnp.zeros_like(acc)

        head = pl.ds(pl.multiple_of((g * 4 + h) * DH, DH), DH)
        here = pl.ds(pl.multiple_of(t * T, T), T)
        q, do = q_s[here, head], do_s[here, head]
        product = do.astype(F32) * o_s[here, head].astype(F32)
        delta = jnp.sum(jnp.transpose(product), axis=0, keepdims=True)
        dq = jnp.zeros((T, DH), F32)
        for c in range(NK):
            dp = dot(kv[2 + g, rows(t, c), :], do, NT)
            ds = (p_ref[n, c].astype(F32) * (dp - delta)).astype(BF)
            acc[rows(t, c), :] += dot(ds, q, NN)
            dq = dq + dot(ds, kv[g, rows(t, c), :], TN)
        dq_s[here, head] = (dq * FACTOR).astype(BF)

        @pl.when(lax.rem(n, 8) == 7)
        def _():
            dkp[g] = (acc[...] * FACTOR).astype(BF)

        return 0

    lax.fori_loop(0, 16, phase2, 0)

    dk_copy = pltpu.make_async_copy(dkp, dk_out, lsem.at[16])
    dk_copy.start()
    for copy in dq_swap(1):
        copy.start()
    dk_copy.wait()
    for g in (0, 1):
        for copy in dq_swap(g) + spread(g) + keep(g):
            copy.wait()
        for k in (1, 2, 3):
            give(g, k).wait_send()

        @pl.when(has_prev)
        def _():
            back(g).wait_send()

    for copy in x_along():
        copy.wait_send()
    for copy in x_forward():
        copy.wait()
    for i in range(7):
        swaps[i].wait_send()
    sg_swap.wait_send()
    for u in range(5):

        @pl.when(has_next)
        def _():
            forth(u).wait_send()

        for k in (1, 2, 3):
            along(u, k, 4).wait_send()


def attend(q, do, o, k, v, sg, x):
    dma = pltpu.SemaphoreType.DMA
    return pl.pallas_call(
        main_kernel,
        in_specs=[ANY] * 5 + [VM, ANY],
        out_specs=[ANY] * 5,
        out_shape=[
            jax.ShapeDtypeStruct((T, 16 * DH), BF),
            jax.ShapeDtypeStruct((T, 4 * DH), BF),
            jax.ShapeDtypeStruct((2, 4, T, 2 * DH), BF),
            jax.ShapeDtypeStruct((2, WIN, DH), BF),
            jax.ShapeDtypeStruct((2, 4, 2, T, 512), BF),
        ],
        scratch_shapes=[
            pltpu.VMEM((CHIP, 8 * DH), BF),
            pltpu.VMEM((CHIP, 8 * DH), BF),
            pltpu.VMEM((CHIP, 8 * DH), BF),
            pltpu.VMEM((4, WIN, DH), BF),
            pltpu.VMEM((5, 2, 8, T), jnp.int32),
            pltpu.VMEM((2, NK, T, T), F32),
            pltpu.VMEM((NK, T, T), F32),
            pltpu.VMEM((16, NK, T, T), BF),
            pltpu.VMEM((WIN, DH), F32),
            pltpu.VMEM((CHIP, 8 * DH), BF),
            pltpu.VMEM((2, WIN, DH), BF),
            pltpu.VMEM((2, WIN, DH), BF),
            pltpu.VMEM((2, 3, CHIP, DH), BF),
            pltpu.VMEM((2, CHIP, DH), BF),
            pltpu.VMEM((2, CHIP, DH), BF),
            pltpu.VMEM((2, 2, T, DH), BF),
            dma((17,)), dma((12,)), dma((12,)), dma((5,)), dma((5,)), dma((5, 3)), dma((5, 3)),
            dma((2, 3)), dma((2, 3)), dma((2,)), dma((2,)),
            dma((2, 3)), dma((2, 3)), dma((3, 2)), dma((3, 2)), dma((4,)), dma((4,)),
        ],
        compiler_params=pltpu.CompilerParams(
            collective_id=0, has_side_effects=True, vmem_limit_bytes=56 << 20
        ),
        cost_estimate=pl.CostEstimate(
            flops=12_000_000_000, bytes_accessed=20_000_000, transcendentals=9_400_000
        ),
        name="attend",
    )(q, do, o, k, v, sg, x)


def finish_kernel(
    xg_in, vx_in, vd_in, w_in, dk_in,
    w_out, in_out, dk_out,
    xg, vx, vd, weight, part, got, summed, far, kgot, kept, kpart, kahead, ktotal,
    lsem, rsend, rrecv, zsend, zrecv, gsend, grecv, hsend, hrecv, psend, precv,
):
    me = lax.axis_index("ctx")
    low = lax.axis_index("dp")
    core = lax.rem(me, 2)
    other = 1 - core
    y = lax.rem(me // 2, 4)
    x = lax.rem(me // 8, 4)
    place = lax.rem(me, 32)
    z = (me // 32) * 4 + low
    partner = me + 1 - 2 * core
    has_next = me < 56
    has_prev = me >= 8

    def row_peer(k):
        return me - 2 * y + 2 * lax.rem(y + k, 4)

    def z_peer(j, c):
        to = lax.rem(z + j, 8)
        return {"dp": lax.rem(to, 4), "ctx": (to // 4) * 32 + place - core + c}, to // 4

    near_next = has_next
    near_prev = has_prev

    barrier = pltpu.get_barrier_semaphore()
    for k in (1, 2, 3):
        signal(barrier, row_peer(k))
    for j in range(8):
        for i in (0, 1):
            if j or i:
                pl.semaphore_signal(
                    barrier,
                    inc=1,
                    device_id=z_peer(j, (core if i == 0 else other))[0],
                    device_id_type=MESH,
                )

    @pl.when(near_next)
    def _():
        signal(barrier, me + 8)

    @pl.when(near_prev)
    def _():
        signal(barrier, me - 8)

    loads = [
        pltpu.make_async_copy(a, b, lsem.at[i])
        for i, (a, b) in enumerate(((vx_in, vx), (xg_in, xg), (vd_in, vd), (w_in, weight)))
    ]
    for copy in loads:
        copy.start()
    keeps = [
        pltpu.make_async_copy(dk_in.at[:, pl.ds(i * W, CHIP), :], kept.at[i], lsem.at[4 + i])
        for i in (0, 1)
    ]
    for copy in keeps:
        copy.start()
    pl.semaphore_wait(barrier, 18 + near_next.astype(jnp.int32) + near_prev.astype(jnp.int32))

    gives = [
        remote(
            dk_in.at[:, pl.ds((4 - k) * CHIP, CHIP), :],
            kgot.at[k - 1],
            gsend.at[k - 1],
            grecv.at[k - 1],
            row_peer(4 - k),
        )
        for k in (1, 2, 3)
    ]
    loads[0].wait()
    loads[1].wait()
    for i in (0, 1):
        acc = jnp.zeros((512, 2 * DH), F32)
        for a in (0, 1):
            for k in range(4):
                acc = acc + dot(xg[a, k, i], vx[a, k], TN)
        part[i] = acc.astype(BF).reshape(4, 128, 2 * DH)
    sends = [
        remote(part.at[:, lax.rem(y + k, 4)], got.at[k - 1], rsend.at[k - 1], rrecv.at[k - 1], row_peer(k))
        for k in (1, 2, 3)
    ]
    for copy in sends + gives:
        copy.start()
    loads[2].wait()
    loads[3].wait()
    for i in range(8):
        in_out[:, i * 512 : (i + 1) * 512] = dot(
            vd[...], weight[i * 512 : (i + 1) * 512, :], NT
        ).astype(BF)
    for copy in sends:
        copy.wait_recv()
    acc = part[:, y].astype(F32)
    for k in range(3):
        acc = acc + got[k].astype(F32)
    summed[...] = acc.astype(BF).reshape(2, 2, 64, 2 * DH)

    copies = []
    for j in range(8):
        for i in (0, 1):
            c = core if i == 0 else other
            peer, high = z_peer(j, c)
            src = summed.at[high, c]
            if j == 0 and i == 0:
                copies.append(pltpu.make_async_copy(src, far.at[0, 0], lsem.at[6]))
            else:
                copies.append(
                    pltpu.make_async_remote_copy(
                        src_ref=src,
                        dst_ref=far.at[i, j],
                        send_sem=zsend.at[i, j],
                        recv_sem=zrecv.at[i, j],
                        device_id=peer,
                        device_id_type=MESH,
                    )
                )
    for copy in copies:
        copy.start()

    for copy in keeps:
        copy.wait()
    for copy in gives:
        copy.wait_recv()
    before = kept[0].astype(F32)
    mine = kept[1].astype(F32)
    for k in (1, 2, 3):
        before = before + jnp.where(y + k >= 4, kgot[k - 1].astype(F32), 0.0)
        mine = mine + jnp.where(y + k < 4, kgot[k - 1].astype(F32), 0.0)
    kpart[...] = before.astype(BF)
    back = remote(kpart, kahead, hsend, hrecv, me - 8)

    @pl.when(has_prev)
    def _():
        back.start()

    for copy in copies:
        copy.wait()
    same = far[0, 0].astype(F32)
    cross = far[1, 0].astype(F32)
    for j in range(1, 8):
        same = same + far[0, j].astype(F32)
        cross = cross + far[1, j].astype(F32)
    w_out[:, : 2 * DH] = jnp.where(core == 0, same, cross)
    w_out[:, 2 * DH :] = jnp.where(core == 0, cross, same)

    @pl.when(has_next)
    def _():
        back.wait_recv()

    @pl.when(jnp.logical_not(has_next))
    def _():
        kahead[...] = jnp.zeros_like(kahead)

    ktotal[...] = (mine + kahead[...].astype(F32)).astype(BF).reshape(2, 2, T, DH)
    swaps = []
    for g in (0, 1):
        columns = pl.ds(pl.multiple_of((core * 2 + g) * DH, DH), DH)
        swaps += [
            remote(ktotal.at[g, other], dk_out.at[:, columns], psend.at[g], precv.at[g], partner),
            pltpu.make_async_copy(ktotal.at[g, core], dk_out.at[:, columns], lsem.at[7 + g]),
        ]
    for copy in swaps:
        copy.start()
    for copy in swaps:
        copy.wait()
    for copy in sends + gives:
        copy.wait_send()

    @pl.when(has_prev)
    def _():
        back.wait_send()


def finish(xg, vx, vd, weight, dk):
    dma = pltpu.SemaphoreType.DMA
    return pl.pallas_call(
        finish_kernel,
        in_specs=[ANY] * 5,
        out_specs=[VM, VM, VM],
        out_shape=[
            jax.ShapeDtypeStruct((64, 4 * DH), F32),
            jax.ShapeDtypeStruct((T, 4096), BF),
            jax.ShapeDtypeStruct((T, 4 * DH), BF),
        ],
        scratch_shapes=[
            pltpu.VMEM((2, 4, 2, T, 512), BF),
            pltpu.VMEM((2, 4, T, 2 * DH), BF),
            pltpu.VMEM((T, 4 * DH), BF),
            pltpu.VMEM((4096, 4 * DH), BF),
            pltpu.VMEM((2, 4, 128, 2 * DH), BF),
            pltpu.VMEM((3, 2, 128, 2 * DH), BF),
            pltpu.VMEM((2, 2, 64, 2 * DH), BF),
            pltpu.VMEM((2, 8, 64, 2 * DH), BF),
            pltpu.VMEM((3, 2, CHIP, DH), BF),
            pltpu.VMEM((2, 2, CHIP, DH), BF),
            pltpu.VMEM((2, CHIP, DH), BF),
            pltpu.VMEM((2, CHIP, DH), BF),
            pltpu.VMEM((2, 2, T, DH), BF),
            dma((9,)), dma((3,)), dma((3,)), dma((2, 8)), dma((2, 8)),
            dma((3,)), dma((3,)), dma, dma, dma((2,)), dma((2,)),
        ],
        compiler_params=pltpu.CompilerParams(
            collective_id=1, has_side_effects=True, vmem_limit_bytes=40 << 20
        ),
        name="finish",
    )(xg, vx, vd, weight, dk)


def on_device(
    inputs, value_weight, query_states, key_states, value_states, attention_out, out_grad, segment_ids
):
    weight = lax.all_gather(value_weight, "ctx", axis=0, tiled=True)
    query_grad, value_delta, value_rows, dk, xg = attend(
        query_states[0],
        out_grad[0],
        attention_out[0],
        key_states[0],
        value_states[0],
        segment_ids,
        inputs[0],
    )
    weight_grad, input_grad, key_grad = finish(xg, value_rows, value_delta, weight, dk)
    return (query_grad[None], key_grad[None], input_grad[None], weight_grad)


def solution(mesh):
    placed = (
        P("dp", "ctx", None),
        P("ctx", None),
        P("dp", "ctx", None),
        P("dp", "ctx", None),
        P("dp", "ctx", None),
        P("dp", "ctx", None),
        P("dp", "ctx", None),
        P("dp", "ctx"),
    )
    return jax.shard_map(
        on_device,
        mesh=mesh,
        in_specs=placed,
        out_specs=(
            P("dp", "ctx", None),
            P("dp", "ctx", None),
            P("dp", "ctx", None),
            P("ctx", None),
        ),
        check_vma=False,
    )
```

time: 1710 us -> 182 us (0.11)
  waiting for transfers between devices: 785 us -> 10.6 us
  loops' own time: 327 us -> 0 us
  local copies, waits for them, and re-layouts: 308 us -> 11.5 us
  Pallas kernels: 0 us -> 145 us
  matrix products: 126 us -> 0 us
  starting transfers between devices: 82 us -> 0.04 us
  other arithmetic: 33.3 us -> 0 us
  blocking collectives: 18.7 us -> 0 us
    unnamed x4 -> x1, waiting for transfers between devices: 470 us -> 0.68 us
    another operation x4 -> x0, loops' own time: 327 us -> none  [the longest x1 327 us: carried_in(): return lax.fori_loop(0, peers, turn, start)]
    dynamic_slice x348 -> x0, local copies, waits for them, and re-layouts: 231 us -> none  [the longest x320 195 us: turn(): new = combine(before, jax.tree.map(lambda part: part[k], everything))]
    ppermute x16 -> x0, waiting for transfers between devices: 157 us -> none  [passed_along(): return lax.ppermute(block, axis, route)]
    pallas_call x0 -> x2, Pallas kernels: none -> 145 us  [the longest x1 102 us: attend(): pl.pallas_call(main_kernel, in_specs=[ANY] * 5 + [VM, ANY], out_specs=[AN...]
    all_gather x1, waiting for transfers between devices: 118 us -> 9.94 us  [on_device(): weight = lax.all_gather(value_weight, 'ctx', axis=0, tiled=True)]
    dot_general x18 -> x0, matrix products: 91.3 us -> none  [the longest x4 27.2 us: attend_group(): jnp.einsum('gqk,gqd->kd', prob_low, grad_group, preferred_element_type=jn...]
    ppermute x16 -> x0, starting transfers between devices: 81.9 us -> none  [passed_along(): return lax.ppermute(block, axis, route)]
  transfers between devices with their start and end apart: 19 -> 1, of which waited for: 19 -> 1; matrix products, arithmetic and copies ran while one was open for 3% -> 0% of each run, Pallas kernels for 0% -> 56%
where the time goes in v3:
time: 182 us
  Pallas kernels  145 us (80%)
  between operations  14.1 us (8%)
  local copies, waits for them, and re-layouts  11.5 us (6%)
  waiting for transfers between devices  10.6 us (6%)
    pallas_call x1, Pallas kernels, attend(): pl.pallas_call(main_kernel, in_specs=[ANY] * 5 + [VM, ANY], out_specs=[AN...  102 us
    pallas_call x1, Pallas kernels, finish(): pl.pallas_call(finish_kernel, in_specs=[ANY] * 5, out_specs=[VM, VM, VM],...  43.8 us
    unnamed x16, local copies, waits for them, and re-layouts  11.5 us
    all_gather x1, waiting for transfers between devices, on_device(): weight = lax.all_gather(value_weight, 'ctx', axis=0, tiled=True)  9.94 us
  transfers between devices with their start and end apart: 1, of which 1 were waited for; matrix products, arithmetic and copies ran while one was open for 0% of the time, Pallas kernels for 56%

profile of v3, /device:TPU:39, one launch (start us, length us, event | category | flops | bytes accessed | tf_op | source)
XLA Modules:
  0.0 181.6 jit_solution(3235803896823780724)
XLA Ops:
  7.2 0.0 all-gather.2.cloned.1.call-start
  7.2 0.7 all-gather.2.cloned.1.call-update
  7.9 101.5 %attend.1 = (bf16[256,2048]{1,0:T(8,128)(2,1)}, bf16[256,512]{1,0:T(8,128)(2,1)}, bf16[2,4,256,256]{3,2,1,0:T(8,128)(2,1)}, bf16[2,2560,128]{2,1,0:T(8,128)(2,1)}, bf16[2,4,2,256,512]{4,3,2,1,0:T(8,128)(2,1)}) custom-call(bf16[256,2048]{1,0:T(8,128)(2,1)} %bitcast.13, bf16[256,2048]{1,0:T(8,128)(2,1)} %bitcast.14, bf16[256,2048]{1,0:T(8,128)(2,1)} %bitcast.15, ...), custom_call_target="tpu_custom_call" | custom-call | flops 12000000000 | bytes 20000000 | tf_op jit(solution)/shard_map/attend/pallas_call | solution.py:427
  109.4 9.9 %all-gather.2.cloned.1.call-done.w_in = bf16[4096,512]{1,0:T(8,128)(2,1)} async-done(((bf16[64,512]{1,0:T(8,128)(2,1)}), bf16[4096,512]{1,0:T(8,128)(2,1)}) %all-gather.2.cloned.1.call-update) | async-done | bytes 4194320 | tf_op jit(solution)/shard_map/all_gather | solution.py:683
  119.4 0.0 copy-start
  119.4 2.2 %copy-done = bf16[4096,512]{1,0:T(8,128)(2,1)S(1)} copy-done((bf16[4096,512]{1,0:T(8,128)(2,1)S(1)}, bf16[4096,512]{1,0:T(8,128)(2,1)}, u32[]{:S(2)}) %copy-start) | copy-done | bytes 4194328
  121.6 0.0 copy-start.1
  121.6 2.2 %copy-done.1 = bf16[2,4,2,256,512]{4,3,2,1,0:T(8,128)(2,1)S(1)} copy-done((bf16[2,4,2,256,512]{4,3,2,1,0:T(8,128)(2,1)S(1)}, bf16[2,4,2,256,512]{4,3,2,1,0:T(8,128)(2,1)}, u32[]{:S(2)}) %copy-start.1) | copy-done | bytes 4194328
  123.7 0.0 copy-start.2
  123.7 1.3 copy-done.2
  125.1 0.0 copy-start.3
  125.1 1.2 copy-done.3
  126.3 0.0 copy-start.4
  126.3 0.9 copy-done.4
  127.2 0.0 copy-start.5
  127.2 43.8 %finish.1 = (f32[64,512]{1,0:T(8,128)S(1)}, bf16[256,4096]{1,0:T(8,128)(2,1)S(1)}, bf16[256,512]{1,0:T(8,128)(2,1)S(1)}) custom-call(bf16[2,4,2,256,512]{4,3,2,1,0:T(8,128)(2,1)S(1)} %copy-done.1, bf16[2,4,256,256]{3,2,1,0:T(8,128)(2,1)S(1)} %copy-done.3, bf16[256,512]{1,0:T(8,128)(2,1)S(1)} %copy-done.4, bf16[4096,512]{1,0:T(8,128)(2,1)S(1)} %copy-done, ...), custom_call_target="tpu_custom_call" | custom-call | tf_op jit(solution)/shard_map/finish/pallas_call | solution.py:647
  171.1 0.0 copy-done.5
  171.1 1.0 copy.16
  172.0 0.7 copy.17
  172.7 1.3 copy.18
  174.1 0.7 copy.19
Async XLA Ops:
  7.2 112.2 %all-gather.2.cloned.1.call-start = ((), (), s32[]{:S(2)}) async-start(), calls=%async_computation | async-start | bytes 4259840 | tf_op jit(solution)/shard_map/all_gather | solution.py:683
  119.4 2.2 %copy-start = (bf16[4096,512]{1,0:T(8,128)(2,1)S(1)}, bf16[4096,512]{1,0:T(8,128)(2,1)}, u32[]{:S(2)}) copy-start(bf16[4096,512]{1,0:T(8,128)(2,1)} %all-gather.2.cloned.1.call-done.w_in) | copy-start | bytes 12582916
  121.6 2.2 %copy-start.1 = (bf16[2,4,2,256,512]{4,3,2,1,0:T(8,128)(2,1)S(1)}, bf16[2,4,2,256,512]{4,3,2,1,0:T(8,128)(2,1)}, u32[]{:S(2)}) copy-start(bf16[2,4,2,256,512]{4,3,2,1,0:T(8,128)(2,1)} %get-tuple-element.13.xg_in) | copy-start | bytes 12582916
  123.7 1.3 copy-start.2
  125.1 1.2 copy-start.3
  126.3 0.9 copy-start.4
  127.2 43.8 %copy-start.5 = (bf16[256,2048]{1,0:T(8,128)(2,1)S(1)}, bf16[256,2048]{1,0:T(8,128)(2,1)}, u32[]{:S(2)}) copy-start(bf16[256,2048]{1,0:T(8,128)(2,1)} %get-tuple-element.12) | copy-start | bytes 3145732
Sparse Core Ops, SparseCore 0:
  11.7 107.6 all-gather.1

commit v4 on v3

v4 whole, which is shorter than its diff:
```python
import math

import jax
import jax.numpy as jnp
from jax import lax
from jax.experimental import pallas as pl
from jax.experimental.pallas import tpu as pltpu
from jax.sharding import PartitionSpec as P

DH = 128
W = 2048
T = 256
CHIP = 2 * T
NK = W // T + 1
WIN = W + CHIP
FACTOR = 1.0 / math.sqrt(DH)
FACTOR2 = FACTOR * math.log2(math.e)
BF = jnp.bfloat16
F32 = jnp.float32
MESH = pl.DeviceIdType.MESH
ANY = pl.BlockSpec(memory_space=pl.ANY)
VM = pl.BlockSpec(memory_space=pltpu.VMEM)
NT = (((1,), (1,)), ((), ()))
NN = (((1,), (0,)), ((), ()))
TN = (((0,), (0,)), ((), ()))


def dot(a, b, dims):
    return lax.dot_general(a, b, dims, preferred_element_type=F32)


def signal(sem, ctx):
    pl.semaphore_signal(sem, inc=1, device_id={"ctx": ctx}, device_id_type=MESH)


def remote(src, dst, send, recv, ctx):
    return pltpu.make_async_remote_copy(
        src_ref=src,
        dst_ref=dst,
        send_sem=send,
        recv_sem=recv,
        device_id={"ctx": ctx},
        device_id_type=MESH,
    )


def main_kernel(
    q_in, do_in, o_in, k_in, v_in, sg_in, x_in, w_in,
    dq_out, dk_out, in_out, w_out, wg,
    q_s, do_s, o_s, kv, sg, bias, s_ref, p_ref, acc, dq_s, gp, got, part, ahead, total,
    vd, vx, xg, wpart, wgot, wsum, far, weight,
    lsem, psend, precv, asend, arecv, rsend, rrecv, gsend, grecv, hsend, hrecv,
    vsend, vrecv, xsend, xrecv, fsend, frecv, ysend, yrecv, zsend, zrecv, wsend, wrecv,
):
    me = lax.axis_index("ctx")
    core = lax.rem(me, 2)
    other = 1 - core
    y = lax.rem(me // 2, 4)
    x = lax.rem(me // 8, 4)
    partner = me + 1 - 2 * core
    has_next = me < 56
    has_prev = me >= 8
    low = lax.axis_index("dp")
    high = me // 32
    place = lax.rem(me, 32)
    far_next = (x == 3) & has_next
    far_prev = (x == 0) & has_prev

    def row_peer(k):
        return me - 2 * y + 2 * lax.rem(y + k, 4)

    def column_peer(k):
        return me - 8 * x + 8 * lax.rem(x + k, 4)

    def z_peer(j, c):
        to = lax.rem(high * 4 + low + j, 8)
        return {"dp": lax.rem(to, 4), "ctx": (to // 4) * 32 + place - core + c}, to // 4

    barrier = pltpu.get_barrier_semaphore()
    for j in range(8):
        for c in (core, other):
            if j or c is other:
                pl.semaphore_signal(
                    barrier, inc=1, device_id=z_peer(j, c)[0], device_id_type=MESH
                )
    for k in (1, 2, 3):
        signal(barrier, row_peer(k))
        signal(barrier, column_peer(k))

    @pl.when(far_next)
    def _():
        signal(barrier, me + 8)

    @pl.when(far_prev)
    def _():
        signal(barrier, me - 8)

    sg[4, core] = jnp.broadcast_to(sg_in[...], (8, T))

    @pl.when(jnp.logical_not(has_prev))
    def _():
        kv[:, :CHIP, :] = jnp.zeros((4, CHIP, DH), BF)
        sg[0] = jnp.full((2, 8, T), -1, jnp.int32)

    pl.semaphore_wait(barrier, 21 + far_next.astype(jnp.int32) + far_prev.astype(jnp.int32))

    half = pl.ds(pl.multiple_of(core * T, T), T)
    rest = pl.ds(pl.multiple_of(other * T, T), T)
    home = pl.ds(pl.multiple_of(W + core * T, T), T)

    def cols(start, n):
        return pl.ds(pl.multiple_of(start * n, n), n)

    def source(i, c):
        if i < 4:
            return (k_in, v_in)[i // 2].at[:, cols(c * 2 + i % 2, DH)]
        return (q_in, do_in, o_in)[i - 4].at[:, cols(c, 8 * DH)]

    def target(i):
        if i < 4:
            return kv.at[i, home, :]
        return (q_s, do_s, o_s)[i - 4].at[half, :]

    swaps = [remote(source(i, other), target(i), psend.at[i], precv.at[i], partner) for i in range(7)]
    stays = [pltpu.make_async_copy(source(i, core), target(i), lsem.at[i]) for i in range(7)]
    sg_swap = remote(sg.at[4, core], sg.at[4, core], psend.at[7], precv.at[7], partner)

    def both(i):
        stays[i].start()
        swaps[i].start()

    both(0)
    sg_swap.start()
    for i in (4, 5, 1, 2, 3, 6):
        both(i)

    def block(u, s):
        if u == 4:
            return sg.at[s]
        return kv.at[u, pl.ds(s * CHIP, CHIP), :]

    def forth(u):
        return remote(block(u, 4), block(u, 0), asend.at[u], arecv.at[u], me + 8)

    def along(u, k, s):
        return remote(
            block(u, s), block(u, 4 - k), rsend.at[u, k - 1], rrecv.at[u, k - 1], row_peer(k)
        )

    def send_own(u):
        if u == 4:
            sg_swap.wait_recv()
        else:
            stays[u].wait()
            swaps[u].wait_recv()

        @pl.when(has_next)
        def _():
            forth(u).start()

        for k in (1, 2, 3):

            @pl.when(y + k < 4)
            def _():
                along(u, k, 4).start()

    def relay(u):
        @pl.when(has_prev)
        def _():
            forth(u).wait_recv()

        for k in (1, 2, 3):

            @pl.when(y + k >= 4)
            def _():
                along(u, k, 0).start()

    def arrived(u):
        for k in (1, 2, 3):
            along(u, k, 4).wait_recv()

    send_own(4)
    send_own(0)
    relay(4)
    relay(0)
    for i in (4, 5):
        stays[i].wait()
        swaps[i].wait_recv()
    arrived(4)

    for i in range(NK + 1):
        sk = jnp.transpose(sg[i // 2, i % 2].astype(F32))[:, :1]
        sk = jnp.broadcast_to(sk, (T, T))
        for t in (0, 1):
            c = i - t
            if 0 <= c < NK:
                live = sk == sg[4, t][:1, :].astype(F32)
                kpos = lax.broadcasted_iota(jnp.int32, (T, T), 0)
                qpos = lax.broadcasted_iota(jnp.int32, (T, T), 1)
                if c == 0:
                    live = live & (kpos > qpos)
                if c == NK - 1:
                    live = live & (kpos <= qpos)
                bias[t, c] = jnp.where(live, 0.0, -1e30)
    arrived(0)

    w_stay = pltpu.make_async_copy(w_in, wg.at[high, x, y, core], lsem.at[17])
    w_swap = remote(w_in, wg.at[high, x, y, core], wsend.at[0], wrecv.at[0], partner)
    w_cross = remote(
        w_in,
        wg.at[high, x, y, core],
        wsend.at[1],
        wrecv.at[1 + core],
        (1 - high) * 32 + place - core + high,
    )

    def w_from(c):
        return remote(w_in, wg.at[high, x, y, c], wsend.at[1], wrecv.at[1 + c], partner)

    def w_x(k):
        return remote(
            wg.at[core, x, y], wg.at[core, x, y], wsend.at[1 + k], wrecv.at[2 + k], column_peer(k)
        )

    def w_y(k):
        return remote(
            wg.at[core, :, y], wg.at[core, :, y], wsend.at[4 + k], wrecv.at[5 + k], row_peer(k)
        )

    w_hand = remote(wg.at[core], wg.at[core], wsend.at[8], wrecv.at[9], partner)

    def w_begin():
        w_cross.start()

        @pl.when(core == high)
        def _():
            w_stay.start()

        @pl.when(core != high)
        def _():
            w_swap.start()

    def w_along_x():
        @pl.when(core == high)
        def _():
            w_stay.wait()
            w_swap.wait_recv()

        @pl.when(core != high)
        def _():
            w_swap.wait_send()
            w_from(0).wait_recv()
            w_from(1).wait_recv()

        for k in (1, 2, 3):
            w_x(k).start()

    def w_along_y():
        for k in (1, 2, 3):
            w_x(k).wait_recv()
        for k in (1, 2, 3):
            w_y(k).start()

    def w_across():
        for k in (1, 2, 3):
            w_y(k).wait_recv()
        w_hand.start()

    w_load = pltpu.make_async_copy(wg, weight, lsem.at[18])

    def w_done():
        w_hand.wait()
        w_cross.wait_send()
        for k in (1, 2, 3):
            w_x(k).wait_send()
            w_y(k).wait_send()
        w_load.start()

    def give(g, k):
        return remote(
            gp.at[g, pl.ds((4 - k) * CHIP, CHIP), :],
            got.at[g, k - 1],
            gsend.at[g, k - 1],
            grecv.at[g, k - 1],
            row_peer(4 - k),
        )

    def back(g):
        return remote(part.at[g], ahead.at[g], hsend.at[g], hrecv.at[g], me - 8)

    def give_start(g):
        for k in (1, 2, 3):
            give(g, k).start()

    def give_sum(g):
        for k in (1, 2, 3):
            give(g, k).wait_recv()
        before = gp[g, :CHIP, :].astype(F32)
        for k in (1, 2, 3):
            before = before + jnp.where(y + k >= 4, got[g, k - 1].astype(F32), 0.0)
        part[g] = before.astype(BF)

        @pl.when(has_prev)
        def _():
            back(g).start()

    def spread(u):
        g = u % 2
        columns = cols(core * 2 + g, DH)
        dst = vd if u < 2 else dk_out
        copies = [
            remote(total.at[u, other], dst.at[:, columns], psend.at[8 + u], precv.at[8 + u], partner)
        ]
        if u < 2:
            copies += [
                remote(
                    total.at[u],
                    vx.at[:, k, :, pl.ds(g * DH, DH)],
                    vsend.at[g, k - 1],
                    vrecv.at[g, k - 1],
                    column_peer(k),
                )
                for k in (1, 2, 3)
            ]
        return copies

    def keep(u):
        g = u % 2
        columns = cols(core * 2 + g, DH)
        if u < 2:
            return [
                pltpu.make_async_copy(total.at[u, core], vd.at[:, columns], lsem.at[8 + u]),
                pltpu.make_async_copy(total.at[u], vx.at[:, 0, :, pl.ds(g * DH, DH)], lsem.at[10 + u]),
            ]
        return [pltpu.make_async_copy(total.at[u, core], dk_out.at[:, columns], lsem.at[8 + u])]

    def give_total(g):
        @pl.when(has_next)
        def _():
            back(g).wait_recv()

        @pl.when(jnp.logical_not(has_next))
        def _():
            ahead[g] = jnp.zeros((CHIP, DH), BF)

        mine = gp[g, W:, :].astype(F32) + ahead[g].astype(F32)
        for k in (1, 2, 3):
            mine = mine + jnp.where(y + k < 4, got[g, k - 1].astype(F32), 0.0)
        total[g] = mine.astype(BF).reshape(2, T, DH)
        for copy in spread(g) + keep(g):
            copy.start()

    def strip(k, high):
        start = pl.multiple_of(high * 2048 + lax.rem(x + k, 4) * 512, 512)
        return x_in.at[:, pl.ds(start, 512)]

    def x_keep():
        return [pltpu.make_async_copy(strip(0, i), xg.at[core, 0, i], lsem.at[12 + i]) for i in (0, 1)]

    def x_along():
        return [
            remote(
                strip(k, i), xg.at[core, k, i], xsend.at[k - 1, i], xrecv.at[k - 1, i], column_peer(k)
            )
            for k in (1, 2, 3)
            for i in (0, 1)
        ]

    def x_forward():
        return [
            remote(xg.at[core, k], xg.at[core, k], fsend.at[k], frecv.at[k], partner) for k in range(4)
        ]

    def at(n, when, *calls):
        @pl.when(n == when)
        def _():
            for f, *args in calls:
                f(*args)

    def start_all(make):
        for copy in make():
            copy.start()

    def x_pass():
        for copy in x_keep():
            copy.wait()
        for copy in x_along():
            copy.wait_recv()
        for copy in x_forward():
            copy.start()

    def w_part():
        for copy in x_forward():
            copy.wait()
        for u in (0, 1):
            for copy in spread(u) + keep(u):
                copy.wait()
        for i in (0, 1):
            sums = jnp.zeros((512, 2 * DH), F32)
            for a in (0, 1):
                for k in range(4):
                    sums = sums + dot(xg[a, k, i], vx[a, k], TN)
            wpart[i] = sums.astype(BF).reshape(4, 128, 2 * DH)
        for copy in y_sends():
            copy.start()

    def y_sends():
        return [
            remote(
                wpart.at[:, lax.rem(y + k, 4)],
                wgot.at[k - 1],
                ysend.at[k - 1],
                yrecv.at[k - 1],
                row_peer(k),
            )
            for k in (1, 2, 3)
        ]

    def z_sends():
        copies = []
        for j in range(8):
            for i in (0, 1):
                peer, part_of = z_peer(j, core if i == 0 else other)
                src = wsum.at[part_of, core if i == 0 else other]
                if j == 0 and i == 0:
                    copies.append(pltpu.make_async_copy(src, far.at[0, 0], lsem.at[7]))
                else:
                    copies.append(
                        pltpu.make_async_remote_copy(
                            src_ref=src,
                            dst_ref=far.at[i, j],
                            send_sem=zsend.at[i, j],
                            recv_sem=zrecv.at[i, j],
                            device_id=peer,
                            device_id_type=MESH,
                        )
                    )
        return copies

    def w_sum():
        for copy in y_sends():
            copy.wait_recv()
        sums = wpart[:, y].astype(F32)
        for k in range(3):
            sums = sums + wgot[k].astype(F32)
        wsum[...] = sums.astype(BF).reshape(2, 2, 64, 2 * DH)
        for copy in z_sends():
            copy.start()

    def w_end():
        for copy in z_sends():
            copy.wait()
        for copy in y_sends():
            copy.wait_send()
        same = far[0, 0].astype(F32)
        cross = far[1, 0].astype(F32)
        for j in range(1, 8):
            same = same + far[0, j].astype(F32)
            cross = cross + far[1, j].astype(F32)
        w_out[:, : 2 * DH] = jnp.where(core == 0, same, cross)
        w_out[:, 2 * DH :] = jnp.where(core == 0, cross, same)

    def rows(t, c):
        return pl.ds(pl.multiple_of(t * T + c * T, T), T)

    def phase1(n, _):
        g, h, t = n // 8, lax.rem(n // 2, 4), lax.rem(n, 2)
        at(n, 0, (send_own, 1), (w_begin,))
        at(n, 3, (relay, 1), (send_own, 2), (w_along_x,), (start_all, x_keep), (start_all, x_along))
        at(n, 8, (arrived, 1), (relay, 2), (send_own, 3), (give_start, 0))
        at(n, 12, (relay, 3))

        @pl.when(lax.rem(n, 8) == 0)
        def _():
            acc[...] = jnp.zeros_like(acc)

        head = pl.ds(pl.multiple_of((g * 4 + h) * DH, DH), DH)
        here = pl.ds(pl.multiple_of(t * T, T), T)
        q, do = q_s[here, head], do_s[here, head]
        top = jnp.full((8, T), -1e30, F32)
        for c in range(NK):
            s = dot(kv[g, rows(t, c), :], q, NT) + bias[t, c]
            s_ref[c] = s
            top = jnp.maximum(top, jnp.max(s.reshape(T // 8, 8, T), axis=0))
        top = jnp.max(top, axis=0, keepdims=True)
        weight = jnp.zeros((8, T), F32)
        for c in range(NK):
            e = jnp.exp2((s_ref[c] - top) * FACTOR2)
            s_ref[c] = e
            weight = weight + jnp.sum(e.reshape(T // 8, 8, T), axis=0)
        inverse = 1.0 / jnp.sum(weight, axis=0, keepdims=True)
        for c in range(NK):
            p = (s_ref[c] * inverse).astype(BF)
            p_ref[n, c] = p
            acc[rows(t, c), :] += dot(p, do, NN)

        @pl.when(lax.rem(n, 8) == 7)
        def _():
            gp[g] = acc[...].astype(BF)

        return 0

    lax.fori_loop(0, 16, phase1, 0)

    def dq_swap(g):
        block = pl.ds(g * 4 * DH, 4 * DH)
        place = cols(core * 2 + g, 4 * DH)
        return [
            remote(dq_s.at[rest, block], dq_out.at[:, place], psend.at[12 + g], precv.at[12 + g], partner),
            pltpu.make_async_copy(dq_s.at[half, block], dq_out.at[:, place], lsem.at[14 + g]),
        ]

    stays[6].wait()
    swaps[6].wait_recv()
    give_start(1)
    arrived(2)

    def phase2(n, _):
        g, h, t = n // 8, lax.rem(n // 2, 4), lax.rem(n, 2)
        at(n, 1, (give_sum, 0))
        at(n, 4, (give_total, 0), (give_sum, 1))
        at(n, 5, (x_pass,), (w_along_y,))
        at(n, 8, (arrived, 3), (give_start, 2))
        at(n, 9, (give_total, 1))
        at(n, 13, (give_sum, 2))

        @pl.when(lax.rem(n, 8) == 0)
        def _():
            acc[...] = jnp.zeros_like(acc)

        head = pl.ds(pl.multiple_of((g * 4 + h) * DH, DH), DH)
        here = pl.ds(pl.multiple_of(t * T, T), T)
        q, do = q_s[here, head], do_s[here, head]
        product = do.astype(F32) * o_s[here, head].astype(F32)
        delta = jnp.sum(jnp.transpose(product), axis=0, keepdims=True)
        for c in range(NK):
            dp = dot(kv[2 + g, rows(t, c), :], do, NT)
            ds = (p_ref[n, c].astype(F32) * (dp - delta)).astype(BF)
            p_ref[n, c] = ds
            acc[rows(t, c), :] += dot(ds, q, NN)

        @pl.when(lax.rem(n, 8) == 7)
        def _():
            gp[2 + g] = (acc[...] * FACTOR).astype(BF)

        return 0

    lax.fori_loop(0, 16, phase2, 0)
    give_start(3)
    w_across()
    w_part()

    def phase3(n, _):
        g, h, t = n // 8, lax.rem(n // 2, 4), lax.rem(n, 2)
        at(n, 3, (give_total, 2))
        at(n, 6, (w_sum,))
        at(n, 8, (start_all, lambda: dq_swap(0)))
        at(n, 10, (give_sum, 3))
        dq = jnp.zeros((T, DH), F32)
        for c in range(NK):
            dq = dq + dot(p_ref[n, c], kv[g, rows(t, c), :], TN)
        head = pl.ds(pl.multiple_of((g * 4 + h) * DH, DH), DH)
        dq_s[pl.ds(pl.multiple_of(t * T, T), T), head] = (dq * FACTOR).astype(BF)
        return 0

    lax.fori_loop(0, 16, phase3, 0)
    for copy in dq_swap(1):
        copy.start()
    w_done()
    w_load.wait()
    for i in range(8):
        a, j = i // 4, i % 4
        rows_of = weight[a, j].reshape(512, 4 * DH)
        in_out[:, i * 512 : (i + 1) * 512] = dot(vd[...], rows_of, NT).astype(BF)
    give_total(3)
    w_end()
    for g in (0, 1):
        for copy in dq_swap(g) + spread(2 + g) + keep(2 + g):
            copy.wait()
    for u in range(4):
        for k in (1, 2, 3):
            give(u, k).wait_send()

        @pl.when(has_prev)
        def _():
            back(u).wait_send()

    for copy in x_along():
        copy.wait_send()
    for i in range(7):
        swaps[i].wait_send()
    sg_swap.wait_send()
    for u in range(5):

        @pl.when(has_next)
        def _():
            forth(u).wait_send()

        for k in (1, 2, 3):
            along(u, k, 4).wait_send()


def attend(q, do, o, k, v, sg, x, w):
    dma = pltpu.SemaphoreType.DMA
    vmem = pltpu.VMEM
    return pl.pallas_call(
        main_kernel,
        in_specs=[ANY] * 5 + [VM, ANY, ANY],
        out_specs=[VM, VM, VM, VM, ANY],
        out_shape=[
            jax.ShapeDtypeStruct((T, 16 * DH), BF),
            jax.ShapeDtypeStruct((T, 4 * DH), BF),
            jax.ShapeDtypeStruct((T, 4096), BF),
            jax.ShapeDtypeStruct((64, 4 * DH), F32),
            jax.ShapeDtypeStruct((2, 4, 4, 2, 64, 4 * DH), BF),
        ],
        scratch_shapes=[
            vmem((CHIP, 8 * DH), BF),
            vmem((CHIP, 8 * DH), BF),
            vmem((CHIP, 8 * DH), BF),
            vmem((4, WIN, DH), BF),
            vmem((5, 2, 8, T), jnp.int32),
            vmem((2, NK, T, T), F32),
            vmem((NK, T, T), F32),
            vmem((16, NK, T, T), BF),
            vmem((WIN, DH), F32),
            vmem((CHIP, 8 * DH), BF),
            vmem((4, WIN, DH), BF),
            vmem((4, 3, CHIP, DH), BF),
            vmem((4, CHIP, DH), BF),
            vmem((4, CHIP, DH), BF),
            vmem((4, 2, T, DH), BF),
            vmem((T, 4 * DH), BF),
            vmem((2, 4, T, 2 * DH), BF),
            vmem((2, 4, 2, T, 512), BF),
            vmem((2, 4, 128, 2 * DH), BF),
            vmem((3, 2, 128, 2 * DH), BF),
            vmem((2, 2, 64, 2 * DH), BF),
            vmem((2, 8, 64, 2 * DH), BF),
            vmem((2, 4, 4, 2, 64, 4 * DH), BF),
            dma((19,)), dma((14,)), dma((14,)), dma((5,)), dma((5,)), dma((5, 3)), dma((5, 3)),
            dma((4, 3)), dma((4, 3)), dma((4,)), dma((4,)),
            dma((2, 3)), dma((2, 3)), dma((3, 2)), dma((3, 2)), dma((4,)), dma((4,)),
            dma((3,)), dma((3,)), dma((2, 8)), dma((2, 8)), dma((9,)), dma((10,)),
        ],
        compiler_params=pltpu.CompilerParams(
            collective_id=0, has_side_effects=True, vmem_limit_bytes=60 << 20
        ),
        name="attend",
    )(q, do, o, k, v, sg, x, w)


def on_device(
    inputs, value_weight, query_states, key_states, value_states, attention_out, out_grad, segment_ids
):
    query_grad, key_grad, input_grad, weight_grad, _ = attend(
        query_states[0],
        out_grad[0],
        attention_out[0],
        key_states[0],
        value_states[0],
        segment_ids,
        inputs[0],
        value_weight,
    )
    return (query_grad[None], key_grad[None], input_grad[None], weight_grad)


def solution(mesh):
    placed = (
        P("dp", "ctx", None),
        P("ctx", None),
        P("dp", "ctx", None),
        P("dp", "ctx", None),
        P("dp", "ctx", None),
        P("dp", "ctx", None),
        P("dp", "ctx", None),
        P("dp", "ctx"),
    )
    return jax.shard_map(
        on_device,
        mesh=mesh,
        in_specs=placed,
        out_specs=(
            P("dp", "ctx", None),
            P("dp", "ctx", None),
            P("dp", "ctx", None),
            P("ctx", None),
        ),
        check_vma=False,
    )
```

time: 182 us -> 151 us (0.83)
  between operations: 14.1 us -> 0.65 us
  waiting for transfers between devices: 10.6 us -> 0 us
  local copies, waits for them, and re-layouts: 11.5 us -> 6.1 us
    all_gather x1 -> x0, waiting for transfers between devices: 9.94 us -> none  [on_device(): weight = lax.all_gather(value_weight, 'ctx', axis=0, tiled=True)]
    unnamed x16 -> x8, local copies, waits for them, and re-layouts: 11.5 us -> 6.1 us
    pallas_call x2 -> x1, Pallas kernels: 145 us -> 144 us  [attend(): pl.pallas_call(main_kernel, in_specs=[ANY] * 5 + [VM, ANY, ANY], out_spec...]
  transfers between devices with their start and end apart: 1 -> 0, of which waited for: 1 -> 0; matrix products, arithmetic and copies ran while one was open for 0% -> 0% of each run, Pallas kernels for 56% -> 0%
where the time goes in v4:
time: 151 us
  Pallas kernels  144 us (95%)
  local copies, waits for them, and re-layouts  6.1 us (4%)
    pallas_call x1, Pallas kernels, attend(): pl.pallas_call(main_kernel, in_specs=[ANY] * 5 + [VM, ANY, ANY], out_spec...  144 us
    unnamed x8, local copies, waits for them, and re-layouts  6.1 us

profile of v4, /device:TPU:39, one launch (start us, length us, event | category | flops | bytes accessed | tf_op | source)
XLA Modules:
  0.0 150.6 jit_solution(11914366988676916045)
XLA Ops:
  0.6 143.8 %attend.1 = (bf16[256,2048]{1,0:T(8,128)(2,1)}, bf16[256,512]{1,0:T(8,128)(2,1)}, bf16[256,4096]{1,0:T(8,128)(2,1)}, f32[64,512]{1,0:T(8,128)}, bf16[2,4,4,2,64,512]{5,4,3,2,1,0:T(8,128)(2,1)}) custom-call(bf16[256,2048]{1,0:T(8,128)(2,1)} %bitcast.11, bf16[256,2048]{1,0:T(8,128)(2,1)} %bitcast.12, bf16[256,2048]{1,0:T(8,128)(2,1)} %bitcast.13, ...), custom_call_target="tpu_custom_call" | custom-call | tf_op jit(solution)/shard_map/attend/pallas_call | solution.py:606
  144.5 0.0 copy-start
  144.5 2.5 %copy.16 = bf16[1,256,2048]{2,1,0:T(8,128)(2,1)} copy(bf16[1,256,2048]{2,1,0:T(8,128)(2,1)} %bitcast.14) | data formatting | bytes 2097152
  146.9 1.7 %copy.17 = bf16[1,256,512]{2,1,0:T(8,128)(2,1)} copy(bf16[1,256,512]{2,1,0:T(8,128)(2,1)} %bitcast.17) | data formatting | bytes 524288
  148.6 0.0 copy-done
  148.6 0.0 copy-start.1
  148.6 1.3 copy.18
  149.9 0.0 copy-done.1
  149.9 0.7 copy.19
Async XLA Ops:
  144.5 4.1 %copy-start = (bf16[256,4096]{1,0:T(8,128)(2,1)S(1)}, bf16[256,4096]{1,0:T(8,128)(2,1)}, u32[]{:S(2)}) copy-start(bf16[256,4096]{1,0:T(8,128)(2,1)} %get-tuple-element.10) | copy-start | bytes 6291460
  148.6 1.3 copy-start.1

commit v5 on v4

--- a/solution.py
+++ b/solution.py
@@ -46,7 +46,7 @@
 
 def main_kernel(
     q_in, do_in, o_in, k_in, v_in, sg_in, x_in, w_in,
-    dq_out, dk_out, in_out, w_out, wg,
+    dq_out, dk_out, in_out, w_out,
     q_s, do_s, o_s, kv, sg, bias, s_ref, p_ref, acc, dq_s, gp, got, part, ahead, total,
     vd, vx, xg, wpart, wgot, wsum, far, weight,
     lsem, psend, precv, asend, arecv, rsend, rrecv, gsend, grecv, hsend, hrecv,
@@ -131,8 +131,8 @@
 
     both(0)
     sg_swap.start()
-    for i in (4, 5, 1, 2, 3, 6):
-        both(i)
+    both(4)
+    both(5)
 
     def block(u, s):
         if u == 4:
@@ -147,7 +147,7 @@
             block(u, s), block(u, 4 - k), rsend.at[u, k - 1], rrecv.at[u, k - 1], row_peer(k)
         )
 
-    def send_own(u):
+    def send_ahead(u):
         if u == 4:
             sg_swap.wait_recv()
         else:
@@ -158,6 +158,7 @@
         def _():
             forth(u).start()
 
+    def send_own(u):
         for k in (1, 2, 3):
 
             @pl.when(y + k < 4)
@@ -179,8 +180,12 @@
         for k in (1, 2, 3):
             along(u, k, 4).wait_recv()
 
+    send_ahead(4)
     send_own(4)
+    send_ahead(0)
     send_own(0)
+    for i in (1, 2, 3, 6):
+        both(i)
     relay(4)
     relay(0)
     for i in (4, 5):
@@ -204,77 +209,82 @@
                 bias[t, c] = jnp.where(live, 0.0, -1e30)
     arrived(0)
 
-    w_stay = pltpu.make_async_copy(w_in, wg.at[high, x, y, core], lsem.at[17])
-    w_swap = remote(w_in, wg.at[high, x, y, core], wsend.at[0], wrecv.at[0], partner)
-    w_cross = remote(
-        w_in,
-        wg.at[high, x, y, core],
-        wsend.at[1],
-        wrecv.at[1 + core],
-        (1 - high) * 32 + place - core + high,
-    )
-
-    def w_from(c):
-        return remote(w_in, wg.at[high, x, y, c], wsend.at[1], wrecv.at[1 + c], partner)
+    zed = high * 4 + low
+
+    def w_at(x_at, y_at, z, c):
+        return weight.at[z // 4, x_at, y_at, c, :, cols(lax.rem(z, 4), DH)]
+
+    every = slice(None)
+    w_mine = w_in.at[:, cols(low, DH)]
+    w_stay = pltpu.make_async_copy(w_mine, w_at(x, y, zed, core), lsem.at[17])
 
     def w_x(k):
         return remote(
-            wg.at[core, x, y], wg.at[core, x, y], wsend.at[1 + k], wrecv.at[2 + k], column_peer(k)
+            w_mine, w_at(x, y, zed, core), wsend.at[k - 1], wrecv.at[k - 1], column_peer(k)
         )
 
     def w_y(k):
-        return remote(
-            wg.at[core, :, y], wg.at[core, :, y], wsend.at[4 + k], wrecv.at[5 + k], row_peer(k)
+        block = w_at(every, y, zed, core)
+        return remote(block, block, wsend.at[2 + k], wrecv.at[2 + k], row_peer(k))
+
+    def w_up(i):
+        block = w_at(every, every, lax.rem(zed + 8 - i, 8), core)
+        return w_round(block, wsend.at[6 + i], wrecv.at[6 + i], 1)
+
+    def w_down(i):
+        block = w_at(every, every, lax.rem(zed + i, 8), core)
+        return w_round(block, wsend.at[10 + i], wrecv.at[10 + i], 7)
+
+    def w_round(block, send, recv, j):
+        return pltpu.make_async_remote_copy(
+            src_ref=block,
+            dst_ref=block,
+            send_sem=send,
+            recv_sem=recv,
+            device_id=z_peer(j, core)[0],
+            device_id_type=MESH,
         )
 
-    w_hand = remote(wg.at[core], wg.at[core], wsend.at[8], wrecv.at[9], partner)
+    w_half = weight.at[:, :, :, core]
+    w_hand = remote(w_half, w_half, wsend.at[13], wrecv.at[13], partner)
 
     def w_begin():
-        w_cross.start()
-
-        @pl.when(core == high)
-        def _():
-            w_stay.start()
-
-        @pl.when(core != high)
-        def _():
-            w_swap.start()
-
-    def w_along_x():
-        @pl.when(core == high)
-        def _():
-            w_stay.wait()
-            w_swap.wait_recv()
-
-        @pl.when(core != high)
-        def _():
-            w_swap.wait_send()
-            w_from(0).wait_recv()
-            w_from(1).wait_recv()
-
+        w_stay.start()
         for k in (1, 2, 3):
             w_x(k).start()
 
     def w_along_y():
+        w_stay.wait()
         for k in (1, 2, 3):
             w_x(k).wait_recv()
         for k in (1, 2, 3):
             w_y(k).start()
 
+    def w_turn(i):
+        if i == 0:
+            for k in (1, 2, 3):
+                w_y(k).wait_recv()
+        else:
+            w_up(i - 1).wait_recv()
+            if i < 4:
+                w_down(i - 1).wait_recv()
+        w_up(i).start()
+        if i < 3:
+            w_down(i).start()
+
     def w_across():
-        for k in (1, 2, 3):
-            w_y(k).wait_recv()
+        w_up(3).wait_recv()
         w_hand.start()
-
-    w_load = pltpu.make_async_copy(wg, weight, lsem.at[18])
 
     def w_done():
         w_hand.wait()
-        w_cross.wait_send()
         for k in (1, 2, 3):
             w_x(k).wait_send()
             w_y(k).wait_send()
-        w_load.start()
+        for i in range(4):
+            w_up(i).wait_send()
+        for i in range(3):
+            w_down(i).wait_send()
 
     def give(g, k):
         return remote(
@@ -357,18 +367,18 @@
     def x_keep():
         return [pltpu.make_async_copy(strip(0, i), xg.at[core, 0, i], lsem.at[12 + i]) for i in (0, 1)]
 
-    def x_along():
+    def x_along(ks=(1, 2, 3)):
         return [
             remote(
                 strip(k, i), xg.at[core, k, i], xsend.at[k - 1, i], xrecv.at[k - 1, i], column_peer(k)
             )
-            for k in (1, 2, 3)
+            for k in ks
             for i in (0, 1)
         ]
 
-    def x_forward():
+    def x_forward(ks=(0, 1, 2, 3)):
         return [
-            remote(xg.at[core, k], xg.at[core, k], fsend.at[k], frecv.at[k], partner) for k in range(4)
+            remote(xg.at[core, k], xg.at[core, k], fsend.at[k], frecv.at[k], partner) for k in ks
         ]
 
     def at(n, when, *calls):
@@ -381,94 +391,96 @@
         for copy in make():
             copy.start()
 
-    def x_pass():
-        for copy in x_keep():
+    def x_pass(*ks):
+        for copy in x_along(ks) if ks[0] else x_keep():
+            copy.wait_recv() if ks[0] else copy.wait()
+        for copy in x_forward(ks):
+            copy.start()
+
+    def w_part(g):
+        if g == 0:
+            for copy in x_forward():
+                copy.wait()
+        for copy in spread(g) + keep(g):
             copy.wait()
-        for copy in x_along():
-            copy.wait_recv()
-        for copy in x_forward():
-            copy.start()
-
-    def w_part():
-        for copy in x_forward():
-            copy.wait()
-        for u in (0, 1):
-            for copy in spread(u) + keep(u):
-                copy.wait()
         for i in (0, 1):
-            sums = jnp.zeros((512, 2 * DH), F32)
+            sums = jnp.zeros((512, DH), F32)
             for a in (0, 1):
                 for k in range(4):
-                    sums = sums + dot(xg[a, k, i], vx[a, k], TN)
-            wpart[i] = sums.astype(BF).reshape(4, 128, 2 * DH)
-        for copy in y_sends():
+                    sums = sums + dot(xg[a, k, i], vx[a, k, :, g * DH : (g + 1) * DH], TN)
+            wpart[g, i] = sums.astype(BF).reshape(4, 128, DH)
+        for copy in y_sends(g):
             copy.start()
 
-    def y_sends():
+    def y_sends(g):
         return [
             remote(
-                wpart.at[:, lax.rem(y + k, 4)],
-                wgot.at[k - 1],
-                ysend.at[k - 1],
-                yrecv.at[k - 1],
+                wpart.at[g, :, lax.rem(y + k, 4)],
+                wgot.at[g, k - 1],
+                ysend.at[g, k - 1],
+                yrecv.at[g, k - 1],
                 row_peer(k),
             )
             for k in (1, 2, 3)
         ]
 
-    def z_sends():
+    def z_sends(g):
         copies = []
         for j in range(8):
             for i in (0, 1):
                 peer, part_of = z_peer(j, core if i == 0 else other)
-                src = wsum.at[part_of, core if i == 0 else other]
+                src = wsum.at[g, part_of, core if i == 0 else other]
                 if j == 0 and i == 0:
-                    copies.append(pltpu.make_async_copy(src, far.at[0, 0], lsem.at[7]))
+                    copies.append(pltpu.make_async_copy(src, far.at[g, 0, 0], lsem.at[18 + g]))
                 else:
                     copies.append(
                         pltpu.make_async_remote_copy(
                             src_ref=src,
-                            dst_ref=far.at[i, j],
-                            send_sem=zsend.at[i, j],
-                            recv_sem=zrecv.at[i, j],
+                            dst_ref=far.at[g, i, j],
+                            send_sem=zsend.at[g, i, j],
+                            recv_sem=zrecv.at[g, i, j],
                             device_id=peer,
                             device_id_type=MESH,
                         )
                     )
         return copies
 
-    def w_sum():
-        for copy in y_sends():
+    def w_sum(g):
+        for copy in y_sends(g):
             copy.wait_recv()
-        sums = wpart[:, y].astype(F32)
+        sums = wpart[g, :, y].astype(F32)
         for k in range(3):
-            sums = sums + wgot[k].astype(F32)
-        wsum[...] = sums.astype(BF).reshape(2, 2, 64, 2 * DH)
-        for copy in z_sends():
+            sums = sums + wgot[g, k].astype(F32)
+        wsum[g] = sums.astype(BF).reshape(2, 2, 64, DH)
+        for copy in z_sends(g):
             copy.start()
 
-    def w_end():
-        for copy in z_sends():
+    def w_end(g):
+        for copy in z_sends(g):
             copy.wait()
-        for copy in y_sends():
+        for copy in y_sends(g):
             copy.wait_send()
-        same = far[0, 0].astype(F32)
-        cross = far[1, 0].astype(F32)
-        for j in range(1, 8):
-            same = same + far[0, j].astype(F32)
-            cross = cross + far[1, j].astype(F32)
-        w_out[:, : 2 * DH] = jnp.where(core == 0, same, cross)
-        w_out[:, 2 * DH :] = jnp.where(core == 0, cross, same)
+        for i in (0, 1):
+            sums = far[g, i, 0].astype(F32)
+            for j in range(1, 8):
+                sums = sums + far[g, i, j].astype(F32)
+            w_out[:, cols((core if i == 0 else other) * 2 + g, DH)] = sums
 
     def rows(t, c):
         return pl.ds(pl.multiple_of(t * T + c * T, T), T)
 
     def phase1(n, _):
         g, h, t = n // 8, lax.rem(n // 2, 4), lax.rem(n, 2)
-        at(n, 0, (send_own, 1), (w_begin,))
-        at(n, 3, (relay, 1), (send_own, 2), (w_along_x,), (start_all, x_keep), (start_all, x_along))
-        at(n, 8, (arrived, 1), (relay, 2), (send_own, 3), (give_start, 0))
-        at(n, 12, (relay, 3))
+        at(n, 0, (send_ahead, 1), (send_own, 1), (send_ahead, 2), (send_ahead, 3), (w_begin,))
+        at(n, 1, (start_all, x_keep), (start_all, lambda: x_along((3,))))
+        at(n, 2, (w_along_y,))
+        at(n, 3, (relay, 1), (send_own, 2), (x_pass, 0))
+        at(n, 5, (start_all, lambda: x_along((1,))))
+        at(n, 6, (relay, 2), (send_own, 3))
+        at(n, 7, (w_turn, 0), (start_all, lambda: x_along((2,))))
+        at(n, 8, (arrived, 1))
+        at(n, 9, (give_start, 0), (relay, 3))
+        at(n, 12, (w_turn, 1), (x_pass, 3))
 
         @pl.when(lax.rem(n, 8) == 0)
         def _():
@@ -518,11 +530,14 @@
     def phase2(n, _):
         g, h, t = n // 8, lax.rem(n // 2, 4), lax.rem(n, 2)
         at(n, 1, (give_sum, 0))
-        at(n, 4, (give_total, 0), (give_sum, 1))
-        at(n, 5, (x_pass,), (w_along_y,))
-        at(n, 8, (arrived, 3), (give_start, 2))
-        at(n, 9, (give_total, 1))
-        at(n, 13, (give_sum, 2))
+        at(n, 2, (w_turn, 2))
+        at(n, 5, (give_total, 0))
+        at(n, 7, (give_sum, 1))
+        at(n, 8, (arrived, 3), (give_start, 2), (x_pass, 1, 2))
+        at(n, 9, (w_turn, 3))
+        at(n, 12, (give_total, 1))
+        at(n, 14, (w_part, 0))
+        at(n, 15, (give_sum, 2))
 
         @pl.when(lax.rem(n, 8) == 0)
         def _():
@@ -548,14 +563,13 @@
     lax.fori_loop(0, 16, phase2, 0)
     give_start(3)
     w_across()
-    w_part()
 
     def phase3(n, _):
         g, h, t = n // 8, lax.rem(n // 2, 4), lax.rem(n, 2)
-        at(n, 3, (give_total, 2))
-        at(n, 6, (w_sum,))
-        at(n, 8, (start_all, lambda: dq_swap(0)))
-        at(n, 10, (give_sum, 3))
+        at(n, 3, (w_sum, 0), (w_part, 1))
+        at(n, 8, (give_total, 2), (start_all, lambda: dq_swap(0)))
+        at(n, 12, (w_sum, 1))
+        at(n, 14, (give_sum, 3))
         dq = jnp.zeros((T, DH), F32)
         for c in range(NK):
             dq = dq + dot(p_ref[n, c], kv[g, rows(t, c), :], TN)
@@ -567,13 +581,13 @@
     for copy in dq_swap(1):
         copy.start()
     w_done()
-    w_load.wait()
     for i in range(8):
         a, j = i // 4, i % 4
         rows_of = weight[a, j].reshape(512, 4 * DH)
         in_out[:, i * 512 : (i + 1) * 512] = dot(vd[...], rows_of, NT).astype(BF)
     give_total(3)
-    w_end()
+    w_end(0)
+    w_end(1)
     for g in (0, 1):
         for copy in dq_swap(g) + spread(2 + g) + keep(2 + g):
             copy.wait()
@@ -606,13 +620,12 @@
     return pl.pallas_call(
         main_kernel,
         in_specs=[ANY] * 5 + [VM, ANY, ANY],
-        out_specs=[VM, VM, VM, VM, ANY],
+        out_specs=[VM] * 4,
         out_shape=[
             jax.ShapeDtypeStruct((T, 16 * DH), BF),
             jax.ShapeDtypeStruct((T, 4 * DH), BF),
             jax.ShapeDtypeStruct((T, 4096), BF),
             jax.ShapeDtypeStruct((64, 4 * DH), F32),
-            jax.ShapeDtypeStruct((2, 4, 4, 2, 64, 4 * DH), BF),
         ],
         scratch_shapes=[
             vmem((CHIP, 8 * DH), BF),
@@ -633,15 +646,15 @@
             vmem((T, 4 * DH), BF),
             vmem((2, 4, T, 2 * DH), BF),
             vmem((2, 4, 2, T, 512), BF),
-            vmem((2, 4, 128, 2 * DH), BF),
-            vmem((3, 2, 128, 2 * DH), BF),
-            vmem((2, 2, 64, 2 * DH), BF),
-            vmem((2, 8, 64, 2 * DH), BF),
+            vmem((2, 2, 4, 128, DH), BF),
+            vmem((2, 3, 2, 128, DH), BF),
+            vmem((2, 2, 2, 64, DH), BF),
+            vmem((2, 2, 8, 64, DH), BF),
             vmem((2, 4, 4, 2, 64, 4 * DH), BF),
-            dma((19,)), dma((14,)), dma((14,)), dma((5,)), dma((5,)), dma((5, 3)), dma((5, 3)),
+            dma((20,)), dma((14,)), dma((14,)), dma((5,)), dma((5,)), dma((5, 3)), dma((5, 3)),
             dma((4, 3)), dma((4, 3)), dma((4,)), dma((4,)),
             dma((2, 3)), dma((2, 3)), dma((3, 2)), dma((3, 2)), dma((4,)), dma((4,)),
-            dma((3,)), dma((3,)), dma((2, 8)), dma((2, 8)), dma((9,)), dma((10,)),
+            dma((2, 3)), dma((2, 3)), dma((2, 2, 8)), dma((2, 2, 8)), dma((14,)), dma((14,)),
         ],
         compiler_params=pltpu.CompilerParams(
             collective_id=0, has_side_effects=True, vmem_limit_bytes=60 << 20
@@ -653,7 +666,7 @@
 def on_device(
     inputs, value_weight, query_states, key_states, value_states, attention_out, out_grad, segment_ids
 ):
-    query_grad, key_grad, input_grad, weight_grad, _ = attend(
+    query_grad, key_grad, input_grad, weight_grad = attend(
         query_states[0],
         out_grad[0],
         attention_out[0],

time: 151 us -> 124 us (0.82)
  Pallas kernels: 144 us -> 117 us
    pallas_call x1, Pallas kernels: 144 us -> 117 us  [attend(): pl.pallas_call(main_kernel, in_specs=[ANY] * 5 + [VM, ANY, ANY], out_spec...]
where the time goes in v5:
time: 124 us
  Pallas kernels  117 us (94%)
  local copies, waits for them, and re-layouts  6.1 us (5%)
    pallas_call x1, Pallas kernels, attend(): pl.pallas_call(main_kernel, in_specs=[ANY] * 5 + [VM, ANY, ANY], out_spec...  117 us
    unnamed x8, local copies, waits for them, and re-layouts  6.1 us

profile of v5, /device:TPU:39, one launch (start us, length us, event | category | flops | bytes accessed | tf_op | source)
XLA Modules:
  0.0 124.1 jit_solution(800276666215920627)
XLA Ops:
  0.6 117.3 %attend.1 = (bf16[256,2048]{1,0:T(8,128)(2,1)}, bf16[256,512]{1,0:T(8,128)(2,1)}, bf16[256,4096]{1,0:T(8,128)(2,1)}, f32[64,512]{1,0:T(8,128)}) custom-call(bf16[256,2048]{1,0:T(8,128)(2,1)} %bitcast.11, bf16[256,2048]{1,0:T(8,128)(2,1)} %bitcast.12, bf16[256,2048]{1,0:T(8,128)(2,1)} %bitcast.13, bf16[256,512]{1,0:T(8,128)(2,1)} %bitcast.15, ...), custom_call_target="tpu_custom_call" | custom-call | tf_op jit(solution)/shard_map/attend/pallas_call | solution.py:620
  117.9 0.0 copy-start
  118.0 2.5 %copy.16 = bf16[1,256,2048]{2,1,0:T(8,128)(2,1)} copy(bf16[1,256,2048]{2,1,0:T(8,128)(2,1)} %bitcast.14) | data formatting | bytes 2097152
  120.4 1.7 %copy.17 = bf16[1,256,512]{2,1,0:T(8,128)(2,1)} copy(bf16[1,256,512]{2,1,0:T(8,128)(2,1)} %bitcast.17) | data formatting | bytes 524288
  122.1 0.0 copy-done
  122.1 0.0 copy-start.1
  122.1 1.3 %copy.18 = bf16[1,256,4096]{2,1,0:T(8,128)(2,1)} copy(bf16[1,256,4096]{2,1,0:T(8,128)(2,1)S(1)} %bitcast.10) | data formatting | bytes 4194304
  123.4 0.0 copy-done.1
  123.4 0.7 copy.19
Async XLA Ops:
  117.9 4.1 %copy-start = (bf16[256,4096]{1,0:T(8,128)(2,1)S(1)}, bf16[256,4096]{1,0:T(8,128)(2,1)}, u32[]{:S(2)}) copy-start(bf16[256,4096]{1,0:T(8,128)(2,1)} %get-tuple-element.10) | copy-start | bytes 6291460
  122.1 1.3 %copy-start.1 = (f32[64,512]{1,0:T(8,128)S(1)}, f32[64,512]{1,0:T(8,128)}, u32[]{:S(2)}) copy-start(f32[64,512]{1,0:T(8,128)} %get-tuple-element.19) | copy-start | bytes 393220

commit v6 on v5

--- a/solution.py
+++ b/solution.py
@@ -471,16 +471,18 @@
 
     def phase1(n, _):
         g, h, t = n // 8, lax.rem(n // 2, 4), lax.rem(n, 2)
-        at(n, 0, (send_ahead, 1), (send_own, 1), (send_ahead, 2), (send_ahead, 3), (w_begin,))
+        at(n, 0, (send_ahead, 1), (send_own, 1), (w_begin,))
         at(n, 1, (start_all, x_keep), (start_all, lambda: x_along((3,))))
-        at(n, 2, (w_along_y,))
+        at(n, 2, (send_ahead, 2), (w_along_y,))
         at(n, 3, (relay, 1), (send_own, 2), (x_pass, 0))
-        at(n, 5, (start_all, lambda: x_along((1,))))
-        at(n, 6, (relay, 2), (send_own, 3))
-        at(n, 7, (w_turn, 0), (start_all, lambda: x_along((2,))))
-        at(n, 8, (arrived, 1))
-        at(n, 9, (give_start, 0), (relay, 3))
-        at(n, 12, (w_turn, 1), (x_pass, 3))
+        at(n, 4, (send_ahead, 3))
+        at(n, 6, (w_turn, 0), (start_all, lambda: x_along((1,))))
+        at(n, 8, (arrived, 1), (relay, 2), (send_own, 3), (start_all, lambda: x_along((2,))))
+        at(n, 9, (give_start, 0))
+        at(n, 10, (w_turn, 1))
+        at(n, 11, (relay, 3))
+        at(n, 12, (x_pass, 3))
+        at(n, 14, (w_turn, 2))
 
         @pl.when(lax.rem(n, 8) == 0)
         def _():
@@ -530,14 +532,13 @@
     def phase2(n, _):
         g, h, t = n // 8, lax.rem(n // 2, 4), lax.rem(n, 2)
         at(n, 1, (give_sum, 0))
-        at(n, 2, (w_turn, 2))
-        at(n, 5, (give_total, 0))
+        at(n, 4, (w_turn, 3))
+        at(n, 6, (give_total, 0))
         at(n, 7, (give_sum, 1))
-        at(n, 8, (arrived, 3), (give_start, 2), (x_pass, 1, 2))
-        at(n, 9, (w_turn, 3))
+        at(n, 8, (arrived, 3), (give_start, 2))
+        at(n, 9, (x_pass, 1, 2))
         at(n, 12, (give_total, 1))
-        at(n, 14, (w_part, 0))
-        at(n, 15, (give_sum, 2))
+        at(n, 15, (w_part, 0), (give_sum, 2))
 
         @pl.when(lax.rem(n, 8) == 0)
         def _():

time: 124 us -> 120 us (0.968)
  Pallas kernels: 117 us -> 112 us
    pallas_call x1, Pallas kernels: 117 us -> 112 us  [attend(): pl.pallas_call(main_kernel, in_specs=[ANY] * 5 + [VM, ANY, ANY], out_spec...]
where the time goes in v6:
time: 120 us; the launch traced here: 119 us
  Pallas kernels  112 us (93%)
  local copies, waits for them, and re-layouts  6.1 us (5%)
    pallas_call x1, Pallas kernels, attend(): pl.pallas_call(main_kernel, in_specs=[ANY] * 5 + [VM, ANY, ANY], out_spec...  112 us
    unnamed x8, local copies, waits for them, and re-layouts  6.1 us

profile of v6, /device:TPU:39, one launch (start us, length us, event | category | flops | bytes accessed | tf_op | source)
XLA Modules:
  0.0 118.8 jit_solution(1959103672278037566)
XLA Ops:
  0.6 112.1 %attend.1 = (bf16[256,2048]{1,0:T(8,128)(2,1)}, bf16[256,512]{1,0:T(8,128)(2,1)}, bf16[256,4096]{1,0:T(8,128)(2,1)}, f32[64,512]{1,0:T(8,128)}) custom-call(bf16[256,2048]{1,0:T(8,128)(2,1)} %bitcast.11, bf16[256,2048]{1,0:T(8,128)(2,1)} %bitcast.12, bf16[256,2048]{1,0:T(8,128)(2,1)} %bitcast.13, bf16[256,512]{1,0:T(8,128)(2,1)} %bitcast.15, ...), custom_call_target="tpu_custom_call" | custom-call | tf_op jit(solution)/shard_map/attend/pallas_call | solution.py:621
  112.7 0.0 copy-start
  112.7 2.5 %copy.16 = bf16[1,256,2048]{2,1,0:T(8,128)(2,1)} copy(bf16[1,256,2048]{2,1,0:T(8,128)(2,1)} %bitcast.14) | data formatting | bytes 2097152
  115.2 1.7 %copy.17 = bf16[1,256,512]{2,1,0:T(8,128)(2,1)} copy(bf16[1,256,512]{2,1,0:T(8,128)(2,1)} %bitcast.17) | data formatting | bytes 524288
  116.9 0.0 copy-done
  116.9 0.0 copy-start.1
  116.9 1.3 %copy.18 = bf16[1,256,4096]{2,1,0:T(8,128)(2,1)} copy(bf16[1,256,4096]{2,1,0:T(8,128)(2,1)S(1)} %bitcast.10) | data formatting | bytes 4194304
  118.2 0.0 copy-done.1
  118.2 0.7 copy.19
Async XLA Ops:
  112.7 4.1 %copy-start = (bf16[256,4096]{1,0:T(8,128)(2,1)S(1)}, bf16[256,4096]{1,0:T(8,128)(2,1)}, u32[]{:S(2)}) copy-start(bf16[256,4096]{1,0:T(8,128)(2,1)} %get-tuple-element.10) | copy-start | bytes 6291460
  116.9 1.3 %copy-start.1 = (f32[64,512]{1,0:T(8,128)S(1)}, f32[64,512]{1,0:T(8,128)}, u32[]{:S(2)}) copy-start(f32[64,512]{1,0:T(8,128)} %get-tuple-element.19) | copy-start | bytes 393220
